TPU v7x, 256 devices: a whole 4x4x8 slice. The times are simulated.
256 devices in a mesh: len: 16 (over y, x_lo, core), wid: 16 (over x_hi, z).
Axes of the slice: x: 4 (x_hi: 2, x_lo: 2; x = x_hi * 2 + x_lo), y: 4, z: 8, core: 2. Of those that a mesh axis runs over, the one named last changes fastest.
Arguments:
- ckpt_e: float32 [3, 256, 256, 128], P(None, 'len', 'wid'), may hold values from -6 to 6
- ckpt_h: float32 [3, 256, 256, 128], P(None, 'len', 'wid'), may hold values from -6 to 6
- adj_e: float32 [3, 256, 256, 128], P(None, 'len', 'wid'), may hold values from -6 to 6
- adj_h: float32 [3, 256, 256, 128], P(None, 'len', 'wid'), may hold values from -6 to 6
- material: int32 [256, 256, 128], P('len', 'wid'), may hold values from 0 to 3
- inv_perm: float32 [4], replicated, may hold values from 0.2 to 1
- poling: int32 [32, 32], P('len', 'wid'), may hold values from 0 to 1
- freqs: float32 [8], replicated, may hold values from 0.1 to 3
Outputs:
- adjoint_e: float32 [3, 256, 256, 128], P(None, 'len', 'wid')
- adjoint_h: float32 [3, 256, 256, 128], P(None, 'len', 'wid')
- gradient: float32 [2, 8, 32, 32], P(None, None, 'len', 'wid')
All inputs are finite; a program needn't handle non-finite values.
Results may differ from a plain program's by a relative error of at most 0.0001.
Values sent between devices are 32-bit elements; how exact they have to be, the bound alone decides.
No kernel may reach another device: no remote copies, remote signals or barrier semaphores. Data moves between devices by JAX's collectives and lax.ppermute only.
A program may use at most 64 MiB of HBM per device.

v0:
```python
import math

import jax
import jax.numpy as jnp
from jax import lax
from jax.sharding import PartitionSpec as P

STEPS = 8
DOMLEN = 8
WBLK = 8


COURANT = 0.5
OMEGA = 0.9


def shifted(value, axis, steps):
    count = lax.axis_size(axis)
    leading, last = (max(0, -steps), min(count, count - steps))
    return lax.ppermute(value, axis, [(source, source + steps) for source in range(leading, last)])


def carried_in(value, axis, join, neutral):
    count, mine = (lax.axis_size(axis), lax.axis_index(axis))
    pieces = lax.all_gather(value, axis)
    total = jnp.full_like(value, 0) + jnp.asarray(neutral, value.dtype)

    def hop(position, total):
        longer = join(total, pieces[position])
        return jnp.where(position < mine, longer, total)

    return lax.fori_loop(0, count - 1, hop, total)


def zdiff_forward(field):
    padded = jnp.pad(field, ((0, 0), (0, 0), (0, 1)))
    return padded[:, :, 1:] - field


def zdiff_backward(field):
    padded = jnp.pad(field, ((0, 0), (0, 0), (1, 0)))
    return field - padded[:, :, :-1]


def xdiff_forward(field, plane):
    return jnp.concatenate([field[1:], plane[None]], axis=0) - field


def ydiff_forward(field, plane):
    return jnp.concatenate([field[:, 1:], plane[:, None]], axis=1) - field


def xdiff_backward(field, plane):
    return field - jnp.concatenate([plane[None], field[:-1]], axis=0)


def ydiff_backward(field, plane):
    return field - jnp.concatenate([plane[:, None], field[:, :-1]], axis=1)


def curl_electric(electric):
    send_len = electric[:, 0]
    send_wid = electric[:, :, 0]
    after_len = shifted(send_len, "len", -1)
    after_wid = shifted(send_wid, "wid", -1)
    ylen_plane, zlen_plane = (after_len[1], after_len[2])
    xwid_plane, zwid_plane = (after_wid[0], after_wid[2])
    comp_x, comp_y, comp_z = (electric[0], electric[1], electric[2])
    return jnp.stack(
        [
            ydiff_forward(comp_z, zwid_plane) - zdiff_forward(comp_y),
            zdiff_forward(comp_x) - xdiff_forward(comp_z, zlen_plane),
            xdiff_forward(comp_y, ylen_plane) - ydiff_forward(comp_x, xwid_plane),
        ]
    )


def curl_magnetic(magnetic):
    send_len = magnetic[:, -1]
    send_wid = magnetic[:, :, -1]
    before_len = shifted(send_len, "len", 1)
    before_wid = shifted(send_wid, "wid", 1)
    ylen_plane, zlen_plane = (before_len[1], before_len[2])
    xwid_plane, zwid_plane = (before_wid[0], before_wid[2])
    comp_x, comp_y, comp_z = (magnetic[0], magnetic[1], magnetic[2])
    return jnp.stack(
        [
            ydiff_backward(comp_z, zwid_plane) - zdiff_backward(comp_y),
            zdiff_backward(comp_x) - xdiff_backward(comp_z, zlen_plane),
            xdiff_backward(comp_y, ylen_plane) - ydiff_backward(comp_x, xwid_plane),
        ]
    )


def add_arrays(earlier, later):
    return earlier + later


def per_device(ckpt_e, ckpt_h, adj_e, adj_h, material, inv_perm, poling, freqs):
    len_cells = material.shape[0]
    wid_cells = material.shape[1]
    depth = material.shape[2]
    inv_eps = jnp.zeros(material.shape, jnp.float32)
    for index in range(inv_perm.shape[0]):
        inv_eps = inv_eps + (material == index).astype(jnp.float32) * inv_perm[index]
    chi = (material == 0).astype(jnp.float32)
    signs = (2 * poling - 1).astype(jnp.float32)
    sign_full = jnp.repeat(jnp.repeat(signs, DOMLEN, axis=0), WBLK, axis=1)
    anchor = lax.axis_index("len") * len_cells
    position = (anchor + jnp.arange(len_cells, dtype=jnp.int32)).astype(jnp.float32)
    phase = math.pi / DOMLEN * position
    terms = jnp.stack([sign_full * jnp.cos(phase)[:, None], sign_full * jnp.sin(phase)[:, None]])
    running = jnp.cumsum(terms, axis=1)
    device_total = running[:, -1]
    prefix = carried_in(device_total, "len", add_arrays, jnp.zeros_like(device_total))
    envelope = (running + prefix[:, None, :]) / math.sqrt(lax.axis_size("len") * len_cells)
    stored = []
    electric, magnetic = (ckpt_e, ckpt_h)
    for moment in range(STEPS):
        magnetic = magnetic - COURANT * curl_electric(electric)
        electric = electric + COURANT * inv_eps * curl_magnetic(magnetic)
        stored.append(electric)
    adjoint_e, adjoint_h = (adj_e, adj_h)
    dom_len = len_cells // DOMLEN
    dom_wid = wid_cells // WBLK
    gradient = jnp.zeros((2, freqs.shape[0], dom_len, dom_wid), jnp.float32)
    scale = 1.0 / math.sqrt(DOMLEN * WBLK * depth)
    for moment in range(STEPS, 0, -1):
        forward_field = stored[moment - 1]
        drive = envelope[0] * math.cos(OMEGA * moment) + envelope[1] * math.sin(OMEGA * moment)
        adjoint_e = adjoint_e + drive[None, :, :, None] * chi * forward_field
        product = chi * jnp.sum(adjoint_e * forward_field, axis=0)
        blocks = product.reshape(dom_len, DOMLEN, dom_wid, WBLK, depth).sum(axis=(1, 3, 4)) * scale
        angles = freqs * moment
        gradient = gradient + jnp.stack(
            [jnp.cos(angles)[:, None, None] * blocks, -jnp.sin(angles)[:, None, None] * blocks]
        )
        adjoint_e = adjoint_e - COURANT * inv_eps * curl_magnetic(adjoint_h)
        adjoint_h = adjoint_h + COURANT * curl_electric(adjoint_e)
    return (adjoint_e, adjoint_h, gradient)


def solution(mesh):
    in_specs = (
        P(None, "len", "wid", None),
        P(None, "len", "wid", None),
        P(None, "len", "wid", None),
        P(None, "len", "wid", None),
        P("len", "wid", None),
        P(),
        P("len", "wid"),
        P(),
    )
    out_specs = (
        P(None, "len", "wid", None),
        P(None, "len", "wid", None),
        P(None, None, "len", "wid"),
    )
    return jax.shard_map(
        per_device, mesh=mesh, in_specs=in_specs, out_specs=out_specs, check_vma=False
    )
```

profile of v0, /device:TPU:7, one launch (start us, length us, event | category | flops | bytes accessed | tf_op | source)
XLA Modules:
  0.0 364.6 jit_solution(15309480614071806359)
XLA Ops:
  1.6 8.3 %collective-permute-start = (f32[3,16,128]{2,1,0:T(8,128)S(1)}, f32[3,16,128]{2,1,0:T(8,128)S(1)}, u32[]{:S(2)}, u32[]{:S(2)}) collective-permute-start(f32[3,16,128]{2,1,0:T(8,128)S(1)} %bitcast.1326), channel_id=1, source_target_pairs={{1,0},{2,1},{3,2},{4,3},{5,4},{6,5},{7,6},{8,7},{9,8},{10,9},{11,1... | collective-permute-start | bytes 73736 | tf_op jit(solution)/shard_map/ppermute | solution.py:20
  10.7 3.0 collective-permute-start.1
  13.7 3.7 %collective-permute-start.33 = (f32[3,16,128]{2,0,1:T(4,128)S(1)}, f32[3,16,128]{2,0,1:T(4,128)S(1)}, u32[]{:S(2)}, u32[]{:S(2)}) collective-permute-start(f32[3,16,128]{2,0,1:T(4,128)S(1)} %bitcast.1300), channel_id=1, source_target_pairs={{0,16},{16,32},{32,48},{48,64},{64,80},{80,96},{96,112},{112,128},... | collective-permute-start | bytes 73736 | tf_op jit(solution)/shard_map/ppermute | solution.py:20
  18.6 1.9 collective-permute-start.32
  22.8 15.8 %all-gather = f32[32,1,16]{2,1,0:T(1,128)S(1)} all-gather(f32[2,1,16]{2,1,0:T(1,128)S(1)} %slice.2186), channel_id=2, replica_groups=mesh['len'=16,'wid'=16] {'len'}, dimensions={0}, use_global_device_ids=true | all-gather | bytes 2176 | tf_op jit(solution)/shard_map/all_gather | solution.py:25
  41.9 2.9 broadcast_select_fusion.1
  46.8 1.9 collective-permute-start.2
  49.2 3.8 %collective-permute-start.3 = (f32[3,16,128]{2,0,1:T(4,128)S(1)}, f32[3,16,128]{2,0,1:T(4,128)S(1)}, u32[]{:S(2)}, u32[]{:S(2)}) collective-permute-start(f32[3,16,128]{2,0,1:T(4,128)S(1)} %bitcast.1303), channel_id=1, source_target_pairs={{0,16},{16,32},{32,48},{48,64},{64,80},{80,96},{96,112},{112,128},... | collective-permute-start | bytes 73736 | tf_op jit(solution)/shard_map/ppermute | solution.py:20
  53.0 2.9 collective-permute-done.2
  56.4 5.9 %collective-permute-start.4 = (f32[3,16,128]{2,1,0:T(8,128)S(1)}, f32[3,16,128]{2,1,0:T(8,128)S(1)}, u32[]{:S(2)}, u32[]{:S(2)}) collective-permute-start(f32[3,16,128]{2,1,0:T(8,128)S(1)} %bitcast.1328), channel_id=1, source_target_pairs={{1,0},{2,1},{3,2},{4,3},{5,4},{6,5},{7,6},{8,7},{9,8},{10,9},{11,1... | collective-permute-start | bytes 73736 | tf_op jit(solution)/shard_map/ppermute | solution.py:20
  62.4 4.0 %collective-permute-start.5 = (f32[3,16,128]{2,1,0:T(8,128)S(1)}, f32[3,16,128]{2,1,0:T(8,128)S(1)}, u32[]{:S(2)}, u32[]{:S(2)}) collective-permute-start(f32[3,16,128]{2,1,0:T(8,128)S(1)} %slice_bitcast_fusion.179), channel_id=1, source_target_pairs={{16,0},{32,16},{48,32},{64,48},{80,64},{96,80},{112,96},{128,112},... | collective-permute-start | bytes 73736 | tf_op jit(solution)/shard_map/ppermute | solution.py:20
  66.7 2.1 collective-permute-done.5
  71.3 1.9 collective-permute-start.7
  73.2 4.3 %collective-permute-done.6 = f32[3,16,128]{2,1,0:T(8,128)S(1)} collective-permute-done((f32[3,16,128]{2,1,0:T(8,128)S(1)}, f32[3,16,128]{2,1,0:T(8,128)S(1)}, u32[]{:S(2)}, u32[]{:S(2)}) %collective-permute-start.6) | collective-permute-done | bytes 24608 | tf_op jit(solution)/shard_map/ppermute | solution.py:20
  78.1 4.6 %collective-permute-start.8 = (f32[3,16,128]{2,1,0:T(8,128)S(1)}, f32[3,16,128]{2,1,0:T(8,128)S(1)}, u32[]{:S(2)}, u32[]{:S(2)}) collective-permute-start(f32[3,16,128]{2,1,0:T(8,128)S(1)} %slice_bitcast_fusion.177), channel_id=1, source_target_pairs={{1,0},{2,1},{3,2},{4,3},{5,4},{6,5},{7,6},{8,7},{9,8},{10,9},{11,1... | collective-permute-start | bytes 73736 | tf_op jit(solution)/shard_map/ppermute | solution.py:20
  82.8 3.5 collective-permute-start.9
  86.5 2.6 collective-permute-done.9
  89.7 1.9 collective-permute-start.10
  91.7 1.9 collective-permute-start.11
  93.6 4.3 %collective-permute-done.10 = f32[3,16,128]{2,1,0:T(8,128)S(1)} collective-permute-done((f32[3,16,128]{2,1,0:T(8,128)S(1)}, f32[3,16,128]{2,1,0:T(8,128)S(1)}, u32[]{:S(2)}, u32[]{:S(2)}) %collective-permute-start.10) | collective-permute-done | bytes 24608 | tf_op jit(solution)/shard_map/ppermute | solution.py:20
  100.3 5.3 %collective-permute-start.12 = (f32[3,16,128]{2,1,0:T(8,128)S(1)}, f32[3,16,128]{2,1,0:T(8,128)S(1)}, u32[]{:S(2)}, u32[]{:S(2)}) collective-permute-start(f32[3,16,128]{2,1,0:T(8,128)S(1)} %slice_bitcast_fusion.174), channel_id=1, source_target_pairs={{1,0},{2,1},{3,2},{4,3},{5,4},{6,5},{7,6},{8,7},{9,8},{10,9},{11,1... | collective-permute-start | bytes 73736 | tf_op jit(solution)/shard_map/ppermute | solution.py:20
  109.0 4.7 %collective-permute-start.15 = (f32[3,16,128]{2,0,1:T(4,128)S(1)}, f32[3,16,128]{2,0,1:T(4,128)S(1)}, u32[]{:S(2)}, u32[]{:S(2)}) collective-permute-start(f32[3,16,128]{2,0,1:T(4,128)S(1)} %bitcast.1306), channel_id=1, source_target_pairs={{0,16},{16,32},{32,48},{48,64},{64,80},{80,96},{96,112},{112,128},... | collective-permute-start | bytes 73736 | tf_op jit(solution)/shard_map/ppermute | solution.py:20
  115.9 3.9 %collective-permute-start.17 = (f32[3,16,128]{2,1,0:T(8,128)S(1)}, f32[3,16,128]{2,1,0:T(8,128)S(1)}, u32[]{:S(2)}, u32[]{:S(2)}) collective-permute-start(f32[3,16,128]{2,1,0:T(8,128)S(1)} %bitcast.1336), channel_id=1, source_target_pairs={{16,0},{32,16},{48,32},{64,48},{80,64},{96,80},{112,96},{128,112},... | collective-permute-start | bytes 73736 | tf_op jit(solution)/shard_map/ppermute | solution.py:20
  119.8 5.4 %collective-permute-start.16 = (f32[3,16,128]{2,1,0:T(8,128)S(1)}, f32[3,16,128]{2,1,0:T(8,128)S(1)}, u32[]{:S(2)}, u32[]{:S(2)}) collective-permute-start(f32[3,16,128]{2,1,0:T(8,128)S(1)} %slice_bitcast_fusion.172), channel_id=1, source_target_pairs={{1,0},{2,1},{3,2},{4,3},{5,4},{6,5},{7,6},{8,7},{9,8},{10,9},{11,1... | collective-permute-start | bytes 73736 | tf_op jit(solution)/shard_map/ppermute | solution.py:20
  128.6 5.4 %collective-permute-start.19 = (f32[3,16,128]{2,0,1:T(4,128)S(1)}, f32[3,16,128]{2,0,1:T(4,128)S(1)}, u32[]{:S(2)}, u32[]{:S(2)}) collective-permute-start(f32[3,16,128]{2,0,1:T(4,128)S(1)} %bitcast.1307), channel_id=1, source_target_pairs={{0,16},{16,32},{32,48},{48,64},{64,80},{80,96},{96,112},{112,128},... | collective-permute-start | bytes 73736 | tf_op jit(solution)/shard_map/ppermute | solution.py:20
  135.8 3.4 collective-permute-start.21
  139.2 6.3 %collective-permute-start.20 = (f32[3,16,128]{2,1,0:T(8,128)S(1)}, f32[3,16,128]{2,1,0:T(8,128)S(1)}, u32[]{:S(2)}, u32[]{:S(2)}) collective-permute-start(f32[3,16,128]{2,1,0:T(8,128)S(1)} %slice_bitcast_fusion.170), channel_id=1, source_target_pairs={{1,0},{2,1},{3,2},{4,3},{5,4},{6,5},{7,6},{8,7},{9,8},{10,9},{11,1... | collective-permute-start | bytes 73736 | tf_op jit(solution)/shard_map/ppermute | solution.py:20
  146.9 1.9 collective-permute-start.22
  148.9 5.4 %collective-permute-start.23 = (f32[3,16,128]{2,0,1:T(4,128)S(1)}, f32[3,16,128]{2,0,1:T(4,128)S(1)}, u32[]{:S(2)}, u32[]{:S(2)}) collective-permute-start(f32[3,16,128]{2,0,1:T(4,128)S(1)} %bitcast.1308), channel_id=1, source_target_pairs={{0,16},{16,32},{32,48},{48,64},{64,80},{80,96},{96,112},{112,128},... | collective-permute-start | bytes 73736 | tf_op jit(solution)/shard_map/ppermute | solution.py:20
  156.2 2.5 collective-permute-start.25
  158.7 7.1 %collective-permute-start.24 = (f32[3,16,128]{2,1,0:T(8,128)S(1)}, f32[3,16,128]{2,1,0:T(8,128)S(1)}, u32[]{:S(2)}, u32[]{:S(2)}) collective-permute-start(f32[3,16,128]{2,1,0:T(8,128)S(1)} %slice_bitcast_fusion.168), channel_id=1, source_target_pairs={{1,0},{2,1},{3,2},{4,3},{5,4},{6,5},{7,6},{8,7},{9,8},{10,9},{11,1... | collective-permute-start | bytes 73736 | tf_op jit(solution)/shard_map/ppermute | solution.py:20
  169.3 5.6 %collective-permute-start.27 = (f32[3,16,128]{2,0,1:T(4,128)S(1)}, f32[3,16,128]{2,0,1:T(4,128)S(1)}, u32[]{:S(2)}, u32[]{:S(2)}) collective-permute-start(f32[3,16,128]{2,0,1:T(4,128)S(1)} %bitcast.1309), channel_id=1, source_target_pairs={{0,16},{16,32},{32,48},{48,64},{64,80},{80,96},{96,112},{112,128},... | collective-permute-start | bytes 73736 | tf_op jit(solution)/shard_map/ppermute | solution.py:20
  176.2 1.9 collective-permute-start.29
  178.2 8.1 %collective-permute-start.28 = (f32[3,16,128]{2,1,0:T(8,128)S(1)}, f32[3,16,128]{2,1,0:T(8,128)S(1)}, u32[]{:S(2)}, u32[]{:S(2)}) collective-permute-start(f32[3,16,128]{2,1,0:T(8,128)S(1)} %slice_bitcast_fusion.166), channel_id=1, source_target_pairs={{1,0},{2,1},{3,2},{4,3},{5,4},{6,5},{7,6},{8,7},{9,8},{10,9},{11,1... | collective-permute-start | bytes 73736 | tf_op jit(solution)/shard_map/ppermute | solution.py:20
  187.8 5.4 %collective-permute-start.31 = (f32[3,16,128]{2,1,0:T(8,128)S(1)}, f32[3,16,128]{2,1,0:T(8,128)S(1)}, u32[]{:S(2)}, u32[]{:S(2)}) collective-permute-start(f32[3,16,128]{2,1,0:T(8,128)S(1)} %bitcast.1329), channel_id=1, source_target_pairs={{0,16},{16,32},{32,48},{48,64},{64,80},{80,96},{96,112},{112,128},... | collective-permute-start | bytes 73736 | tf_op jit(solution)/shard_map/ppermute | solution.py:20
  195.2 7.4 %collective-permute-done.30 = f32[3,16,128]{2,1,0:T(8,128)S(1)} collective-permute-done((f32[3,16,128]{2,1,0:T(8,128)S(1)}, f32[3,16,128]{2,1,0:T(8,128)S(1)}, u32[]{:S(2)}, u32[]{:S(2)}) %collective-permute-start.30) | collective-permute-done | bytes 24608 | tf_op jit(solution)/shard_map/ppermute | solution.py:20
  204.1 3.4 collective-permute-start.34
  209.4 4.2 %collective-permute-done.35 = f32[3,16,128]{2,0,1:T(4,128)S(1)} collective-permute-done((f32[3,16,128]{2,0,1:T(4,128)S(1)}, f32[3,16,128]{2,0,1:T(4,128)S(1)}, u32[]{:S(2)}, u32[]{:S(2)}) %collective-permute-start.35) | collective-permute-done | bytes 24608 | tf_op jit(solution)/shard_map/ppermute | solution.py:20
  214.1 1.9 collective-permute-start.37
  216.1 1.9 collective-permute-start.36
  218.1 6.2 %collective-permute-done.36 = f32[3,16,128]{2,1,0:T(8,128)S(1)} collective-permute-done((f32[3,16,128]{2,1,0:T(8,128)S(1)}, f32[3,16,128]{2,1,0:T(8,128)S(1)}, u32[]{:S(2)}, u32[]{:S(2)}) %collective-permute-start.36) | collective-permute-done | bytes 24608 | tf_op jit(solution)/shard_map/ppermute | solution.py:20
  224.7 3.6 collective-permute-start.39
  230.9 2.0 collective-permute-done.38
  233.6 4.1 %collective-permute-start.41 = (f32[3,16,128]{2,0,1:T(4,128)S(1)}, f32[3,16,128]{2,0,1:T(4,128)S(1)}, u32[]{:S(2)}, u32[]{:S(2)}) collective-permute-start(f32[3,16,128]{2,0,1:T(4,128)S(1)} %bitcast.1302), channel_id=1, source_target_pairs={{0,16},{16,32},{32,48},{48,64},{64,80},{80,96},{96,112},{112,128},... | collective-permute-start | bytes 73736 | tf_op jit(solution)/shard_map/ppermute | solution.py:20
  239.7 6.2 %collective-permute-done.40 = f32[3,16,128]{2,1,0:T(8,128)S(1)} collective-permute-done((f32[3,16,128]{2,1,0:T(8,128)S(1)}, f32[3,16,128]{2,1,0:T(8,128)S(1)}, u32[]{:S(2)}, u32[]{:S(2)}) %collective-permute-start.40) | collective-permute-done | bytes 24608 | tf_op jit(solution)/shard_map/ppermute | solution.py:20
  246.5 2.1 collective-permute-start.43
  248.6 2.1 collective-permute-start.42
  253.7 5.5 %collective-permute-start.45 = (f32[3,16,128]{2,1,0:T(8,128)S(1)}, f32[3,16,128]{2,1,0:T(8,128)S(1)}, u32[]{:S(2)}, u32[]{:S(2)}) collective-permute-start(f32[3,16,128]{2,1,0:T(8,128)S(1)} %bitcast.1330), channel_id=1, source_target_pairs={{0,16},{16,32},{32,48},{48,64},{64,80},{80,96},{96,112},{112,128},... | collective-permute-start | bytes 73736 | tf_op jit(solution)/shard_map/ppermute | solution.py:20
  261.2 6.2 %collective-permute-done.44 = f32[3,16,128]{2,1,0:T(8,128)S(1)} collective-permute-done((f32[3,16,128]{2,1,0:T(8,128)S(1)}, f32[3,16,128]{2,1,0:T(8,128)S(1)}, u32[]{:S(2)}, u32[]{:S(2)}) %collective-permute-start.44) | collective-permute-done | bytes 24608 | tf_op jit(solution)/shard_map/ppermute | solution.py:20
  269.8 2.2 collective-permute-start.46
  275.0 5.7 %collective-permute-start.49 = (f32[3,16,128]{2,0,1:T(4,128)S(1)}, f32[3,16,128]{2,0,1:T(4,128)S(1)}, u32[]{:S(2)}, u32[]{:S(2)}) collective-permute-start(f32[3,16,128]{2,0,1:T(4,128)S(1)} %bitcast.1301), channel_id=1, source_target_pairs={{0,16},{16,32},{32,48},{48,64},{64,80},{80,96},{96,112},{112,128},... | collective-permute-start | bytes 73736 | tf_op jit(solution)/shard_map/ppermute | solution.py:20
  282.7 6.2 %collective-permute-done.48 = f32[3,16,128]{2,1,0:T(8,128)S(1)} collective-permute-done((f32[3,16,128]{2,1,0:T(8,128)S(1)}, f32[3,16,128]{2,1,0:T(8,128)S(1)}, u32[]{:S(2)}, u32[]{:S(2)}) %collective-permute-start.48) | collective-permute-done | bytes 24608 | tf_op jit(solution)/shard_map/ppermute | solution.py:20
  291.4 2.2 collective-permute-start.50
  296.3 5.7 %collective-permute-start.53 = (f32[3,16,128]{2,1,0:T(8,128)S(1)}, f32[3,16,128]{2,1,0:T(8,128)S(1)}, u32[]{:S(2)}, u32[]{:S(2)}) collective-permute-start(f32[3,16,128]{2,1,0:T(8,128)S(1)} %bitcast.1331), channel_id=1, source_target_pairs={{0,16},{16,32},{32,48},{48,64},{64,80},{80,96},{96,112},{112,128},... | collective-permute-start | bytes 73736 | tf_op jit(solution)/shard_map/ppermute | solution.py:20
  302.1 1.9 collective-permute-start.52
  304.0 6.2 %collective-permute-done.52 = f32[3,16,128]{2,1,0:T(8,128)S(1)} collective-permute-done((f32[3,16,128]{2,1,0:T(8,128)S(1)}, f32[3,16,128]{2,1,0:T(8,128)S(1)}, u32[]{:S(2)}, u32[]{:S(2)}) %collective-permute-start.52) | collective-permute-done | bytes 24608 | tf_op jit(solution)/shard_map/ppermute | solution.py:20
  312.8 2.2 collective-permute-start.54
  319.9 5.7 %collective-permute-start.57 = (f32[3,16,128]{2,1,0:T(8,128)S(1)}, f32[3,16,128]{2,1,0:T(8,128)S(1)}, u32[]{:S(2)}, u32[]{:S(2)}) collective-permute-start(f32[3,16,128]{2,1,0:T(8,128)S(1)} %slice_bitcast_fusion.152), channel_id=1, source_target_pairs={{0,16},{16,32},{32,48},{48,64},{64,80},{80,96},{96,112},{112,128},... | collective-permute-start | bytes 73736 | tf_op jit(solution)/shard_map/ppermute | solution.py:20
  327.1 7.9 %collective-permute-start.58 = (f32[3,16,128]{2,1,0:T(8,128)S(1)}, f32[3,16,128]{2,1,0:T(8,128)S(1)}, u32[]{:S(2)}, u32[]{:S(2)}) collective-permute-start(f32[3,16,128]{2,1,0:T(8,128)S(1)} %bitcast.1327), channel_id=1, source_target_pairs={{1,0},{2,1},{3,2},{4,3},{5,4},{6,5},{7,6},{8,7},{9,8},{10,9},{11,1... | collective-permute-start | bytes 73736 | tf_op jit(solution)/shard_map/ppermute | solution.py:20
  341.7 1.9 collective-permute-start.60
  343.7 4.3 %collective-permute-start.61 = (f32[3,16,128]{2,1,0:T(8,128)S(1)}, f32[3,16,128]{2,1,0:T(8,128)S(1)}, u32[]{:S(2)}, u32[]{:S(2)}) collective-permute-start(f32[3,16,128]{2,1,0:T(8,128)S(1)} %slice_bitcast_fusion.150), channel_id=1, source_target_pairs={{0,16},{16,32},{32,48},{48,64},{64,80},{80,96},{96,112},{112,128},... | collective-permute-start | bytes 73736 | tf_op jit(solution)/shard_map/ppermute | solution.py:20
  347.9 2.0 collective-permute-done.60
  350.3 6.8 %collective-permute-start.62 = (f32[3,16,128]{2,1,0:T(8,128)S(1)}, f32[3,16,128]{2,1,0:T(8,128)S(1)}, u32[]{:S(2)}, u32[]{:S(2)}) collective-permute-start(f32[3,16,128]{2,1,0:T(8,128)S(1)} %bitcast.1332), channel_id=1, source_target_pairs={{1,0},{2,1},{3,2},{4,3},{5,4},{6,5},{7,6},{8,7},{9,8},{10,9},{11,1... | collective-permute-start | bytes 73736 | tf_op jit(solution)/shard_map/ppermute | solution.py:20
  359.1 4.3 %collective-permute-done.63 = f32[3,16,128]{2,1,0:T(8,128)S(1)} collective-permute-done((f32[3,16,128]{2,1,0:T(8,128)S(1)}, f32[3,16,128]{2,1,0:T(8,128)S(1)}, u32[]{:S(2)}, u32[]{:S(2)}) %collective-permute-start.63) | collective-permute-done | bytes 24608 | tf_op jit(solution)/shard_map/ppermute | solution.py:20
  (567 shorter events, 85.5 us)
Async XLA Ops:
  1.6 43.9 %collective-permute-start = (f32[3,16,128]{2,1,0:T(8,128)S(1)}, f32[3,16,128]{2,1,0:T(8,128)S(1)}, u32[]{:S(2)}, u32[]{:S(2)}) collective-permute-start(f32[3,16,128]{2,1,0:T(8,128)S(1)} %bitcast.1326), channel_id=1, source_target_pairs={{1,0},{2,1},{3,2},{4,3},{5,4},{6,5},{7,6},{8,7},{9,8},{10,9},{11,1... | collective-permute-start | bytes 73736 | tf_op jit(solution)/shard_map/ppermute | solution.py:20
  10.7 34.8 %collective-permute-start.1 = (f32[3,16,128]{2,1,0:T(8,128)S(1)}, f32[3,16,128]{2,1,0:T(8,128)S(1)}, u32[]{:S(2)}, u32[]{:S(2)}) collective-permute-start(f32[3,16,128]{2,1,0:T(8,128)S(1)} %slice_bitcast_fusion.181), channel_id=1, source_target_pairs={{16,0},{32,16},{48,32},{64,48},{80,64},{96,80},{112,96},{128,112},... | collective-permute-start | bytes 73736 | tf_op jit(solution)/shard_map/ppermute | solution.py:20
  13.7 35.1 %collective-permute-start.33 = (f32[3,16,128]{2,0,1:T(4,128)S(1)}, f32[3,16,128]{2,0,1:T(4,128)S(1)}, u32[]{:S(2)}, u32[]{:S(2)}) collective-permute-start(f32[3,16,128]{2,0,1:T(4,128)S(1)} %bitcast.1300), channel_id=1, source_target_pairs={{0,16},{16,32},{32,48},{48,64},{64,80},{80,96},{96,112},{112,128},... | collective-permute-start | bytes 73736 | tf_op jit(solution)/shard_map/ppermute | solution.py:20
  18.6 30.2 %collective-permute-start.32 = (f32[3,16,128]{2,1,0:T(8,128)S(1)}, f32[3,16,128]{2,1,0:T(8,128)S(1)}, u32[]{:S(2)}, u32[]{:S(2)}) collective-permute-start(f32[3,16,128]{2,1,0:T(8,128)S(1)} %slice_bitcast_fusion.164), channel_id=1, source_target_pairs={{0,1},{1,2},{2,3},{3,4},{4,5},{5,6},{6,7},{7,8},{8,9},{9,10},{10,1... | collective-permute-start | bytes 73736 | tf_op jit(solution)/shard_map/ppermute | solution.py:20
  46.8 9.1 %collective-permute-start.2 = (f32[3,16,128]{2,1,0:T(8,128)S(1)}, f32[3,16,128]{2,1,0:T(8,128)S(1)}, u32[]{:S(2)}, u32[]{:S(2)}) collective-permute-start(f32[3,16,128]{2,1,0:T(8,128)S(1)} %slice_bitcast_fusion.180), channel_id=1, source_target_pairs={{0,1},{1,2},{2,3},{3,4},{4,5},{5,6},{6,7},{7,8},{8,9},{9,10},{10,1... | collective-permute-start | bytes 73736 | tf_op jit(solution)/shard_map/ppermute | solution.py:20
  49.2 6.7 %collective-permute-start.3 = (f32[3,16,128]{2,0,1:T(4,128)S(1)}, f32[3,16,128]{2,0,1:T(4,128)S(1)}, u32[]{:S(2)}, u32[]{:S(2)}) collective-permute-start(f32[3,16,128]{2,0,1:T(4,128)S(1)} %bitcast.1303), channel_id=1, source_target_pairs={{0,16},{16,32},{32,48},{48,64},{64,80},{80,96},{96,112},{112,128},... | collective-permute-start | bytes 73736 | tf_op jit(solution)/shard_map/ppermute | solution.py:20
  56.4 10.2 %collective-permute-start.4 = (f32[3,16,128]{2,1,0:T(8,128)S(1)}, f32[3,16,128]{2,1,0:T(8,128)S(1)}, u32[]{:S(2)}, u32[]{:S(2)}) collective-permute-start(f32[3,16,128]{2,1,0:T(8,128)S(1)} %bitcast.1328), channel_id=1, source_target_pairs={{1,0},{2,1},{3,2},{4,3},{5,4},{6,5},{7,6},{8,7},{9,8},{10,9},{11,1... | collective-permute-start | bytes 73736 | tf_op jit(solution)/shard_map/ppermute | solution.py:20
  62.4 6.3 %collective-permute-start.5 = (f32[3,16,128]{2,1,0:T(8,128)S(1)}, f32[3,16,128]{2,1,0:T(8,128)S(1)}, u32[]{:S(2)}, u32[]{:S(2)}) collective-permute-start(f32[3,16,128]{2,1,0:T(8,128)S(1)} %slice_bitcast_fusion.179), channel_id=1, source_target_pairs={{16,0},{32,16},{48,32},{64,48},{80,64},{96,80},{112,96},{128,112},... | collective-permute-start | bytes 73736 | tf_op jit(solution)/shard_map/ppermute | solution.py:20
  69.3 8.2 %collective-permute-start.6 = (f32[3,16,128]{2,1,0:T(8,128)S(1)}, f32[3,16,128]{2,1,0:T(8,128)S(1)}, u32[]{:S(2)}, u32[]{:S(2)}) collective-permute-start(f32[3,16,128]{2,1,0:T(8,128)S(1)} %slice_bitcast_fusion.178), channel_id=1, source_target_pairs={{0,1},{1,2},{2,3},{3,4},{4,5},{5,6},{6,7},{7,8},{8,9},{9,10},{10,1... | collective-permute-start | bytes 73736 | tf_op jit(solution)/shard_map/ppermute | solution.py:20
  71.3 6.2 %collective-permute-start.7 = (f32[3,16,128]{2,0,1:T(4,128)S(1)}, f32[3,16,128]{2,0,1:T(4,128)S(1)}, u32[]{:S(2)}, u32[]{:S(2)}) collective-permute-start(f32[3,16,128]{2,0,1:T(4,128)S(1)} %bitcast.1304), channel_id=1, source_target_pairs={{0,16},{16,32},{32,48},{48,64},{64,80},{80,96},{96,112},{112,128},... | collective-permute-start | bytes 73736 | tf_op jit(solution)/shard_map/ppermute | solution.py:20
  78.1 8.3 %collective-permute-start.8 = (f32[3,16,128]{2,1,0:T(8,128)S(1)}, f32[3,16,128]{2,1,0:T(8,128)S(1)}, u32[]{:S(2)}, u32[]{:S(2)}) collective-permute-start(f32[3,16,128]{2,1,0:T(8,128)S(1)} %slice_bitcast_fusion.177), channel_id=1, source_target_pairs={{1,0},{2,1},{3,2},{4,3},{5,4},{6,5},{7,6},{8,7},{9,8},{10,9},{11,1... | collective-permute-start | bytes 73736 | tf_op jit(solution)/shard_map/ppermute | solution.py:20
  82.8 6.3 %collective-permute-start.9 = (f32[3,16,128]{2,1,0:T(8,128)S(1)}, f32[3,16,128]{2,1,0:T(8,128)S(1)}, u32[]{:S(2)}, u32[]{:S(2)}) collective-permute-start(f32[3,16,128]{2,1,0:T(8,128)S(1)} %slice_bitcast_fusion.176), channel_id=1, source_target_pairs={{16,0},{32,16},{48,32},{64,48},{80,64},{96,80},{112,96},{128,112},... | collective-permute-start | bytes 73736 | tf_op jit(solution)/shard_map/ppermute | solution.py:20
  89.7 8.2 %collective-permute-start.10 = (f32[3,16,128]{2,1,0:T(8,128)S(1)}, f32[3,16,128]{2,1,0:T(8,128)S(1)}, u32[]{:S(2)}, u32[]{:S(2)}) collective-permute-start(f32[3,16,128]{2,1,0:T(8,128)S(1)} %slice_bitcast_fusion.175), channel_id=1, source_target_pairs={{0,1},{1,2},{2,3},{3,4},{4,5},{5,6},{6,7},{7,8},{8,9},{9,10},{10,1... | collective-permute-start | bytes 73736 | tf_op jit(solution)/shard_map/ppermute | solution.py:20
  91.7 6.2 %collective-permute-start.11 = (f32[3,16,128]{2,0,1:T(4,128)S(1)}, f32[3,16,128]{2,0,1:T(4,128)S(1)}, u32[]{:S(2)}, u32[]{:S(2)}) collective-permute-start(f32[3,16,128]{2,0,1:T(4,128)S(1)} %bitcast.1305), channel_id=1, source_target_pairs={{0,16},{16,32},{32,48},{48,64},{64,80},{80,96},{96,112},{112,128},... | collective-permute-start | bytes 73736 | tf_op jit(solution)/shard_map/ppermute | solution.py:20
  98.4 7.3 %collective-permute-start.13 = (f32[3,16,128]{2,1,0:T(8,128)S(1)}, f32[3,16,128]{2,1,0:T(8,128)S(1)}, u32[]{:S(2)}, u32[]{:S(2)}) collective-permute-start(f32[3,16,128]{2,1,0:T(8,128)S(1)} %bitcast.1335), channel_id=1, source_target_pairs={{16,0},{32,16},{48,32},{64,48},{80,64},{96,80},{112,96},{128,112},... | collective-permute-start | bytes 73736 | tf_op jit(solution)/shard_map/ppermute | solution.py:20
  100.3 6.2 %collective-permute-start.12 = (f32[3,16,128]{2,1,0:T(8,128)S(1)}, f32[3,16,128]{2,1,0:T(8,128)S(1)}, u32[]{:S(2)}, u32[]{:S(2)}) collective-permute-start(f32[3,16,128]{2,1,0:T(8,128)S(1)} %slice_bitcast_fusion.174), channel_id=1, source_target_pairs={{1,0},{2,1},{3,2},{4,3},{5,4},{6,5},{7,6},{8,7},{9,8},{10,9},{11,1... | collective-permute-start | bytes 73736 | tf_op jit(solution)/shard_map/ppermute | solution.py:20
  107.0 8.5 %collective-permute-start.14 = (f32[3,16,128]{2,1,0:T(8,128)S(1)}, f32[3,16,128]{2,1,0:T(8,128)S(1)}, u32[]{:S(2)}, u32[]{:S(2)}) collective-permute-start(f32[3,16,128]{2,1,0:T(8,128)S(1)} %slice_bitcast_fusion.173), channel_id=1, source_target_pairs={{0,1},{1,2},{2,3},{3,4},{4,5},{5,6},{6,7},{7,8},{8,9},{9,10},{10,1... | collective-permute-start | bytes 73736 | tf_op jit(solution)/shard_map/ppermute | solution.py:20
  109.0 6.5 %collective-permute-start.15 = (f32[3,16,128]{2,0,1:T(4,128)S(1)}, f32[3,16,128]{2,0,1:T(4,128)S(1)}, u32[]{:S(2)}, u32[]{:S(2)}) collective-permute-start(f32[3,16,128]{2,0,1:T(4,128)S(1)} %bitcast.1306), channel_id=1, source_target_pairs={{0,16},{16,32},{32,48},{48,64},{64,80},{80,96},{96,112},{112,128},... | collective-permute-start | bytes 73736 | tf_op jit(solution)/shard_map/ppermute | solution.py:20
  115.9 9.4 %collective-permute-start.17 = (f32[3,16,128]{2,1,0:T(8,128)S(1)}, f32[3,16,128]{2,1,0:T(8,128)S(1)}, u32[]{:S(2)}, u32[]{:S(2)}) collective-permute-start(f32[3,16,128]{2,1,0:T(8,128)S(1)} %bitcast.1336), channel_id=1, source_target_pairs={{16,0},{32,16},{48,32},{64,48},{80,64},{96,80},{112,96},{128,112},... | collective-permute-start | bytes 73736 | tf_op jit(solution)/shard_map/ppermute | solution.py:20
  119.8 6.3 %collective-permute-start.16 = (f32[3,16,128]{2,1,0:T(8,128)S(1)}, f32[3,16,128]{2,1,0:T(8,128)S(1)}, u32[]{:S(2)}, u32[]{:S(2)}) collective-permute-start(f32[3,16,128]{2,1,0:T(8,128)S(1)} %slice_bitcast_fusion.172), channel_id=1, source_target_pairs={{1,0},{2,1},{3,2},{4,3},{5,4},{6,5},{7,6},{8,7},{9,8},{10,9},{11,1... | collective-permute-start | bytes 73736 | tf_op jit(solution)/shard_map/ppermute | solution.py:20
  126.6 8.8 %collective-permute-start.18 = (f32[3,16,128]{2,1,0:T(8,128)S(1)}, f32[3,16,128]{2,1,0:T(8,128)S(1)}, u32[]{:S(2)}, u32[]{:S(2)}) collective-permute-start(f32[3,16,128]{2,1,0:T(8,128)S(1)} %slice_bitcast_fusion.171), channel_id=1, source_target_pairs={{0,1},{1,2},{2,3},{3,4},{4,5},{5,6},{6,7},{7,8},{8,9},{9,10},{10,1... | collective-permute-start | bytes 73736 | tf_op jit(solution)/shard_map/ppermute | solution.py:20
  128.6 6.8 %collective-permute-start.19 = (f32[3,16,128]{2,0,1:T(4,128)S(1)}, f32[3,16,128]{2,0,1:T(4,128)S(1)}, u32[]{:S(2)}, u32[]{:S(2)}) collective-permute-start(f32[3,16,128]{2,0,1:T(4,128)S(1)} %bitcast.1307), channel_id=1, source_target_pairs={{0,16},{16,32},{32,48},{48,64},{64,80},{80,96},{96,112},{112,128},... | collective-permute-start | bytes 73736 | tf_op jit(solution)/shard_map/ppermute | solution.py:20
  135.8 9.7 %collective-permute-start.21 = (f32[3,16,128]{2,1,0:T(8,128)S(1)}, f32[3,16,128]{2,1,0:T(8,128)S(1)}, u32[]{:S(2)}, u32[]{:S(2)}) collective-permute-start(f32[3,16,128]{2,1,0:T(8,128)S(1)} %bitcast.1337), channel_id=1, source_target_pairs={{16,0},{32,16},{48,32},{64,48},{80,64},{96,80},{112,96},{128,112},... | collective-permute-start | bytes 73736 | tf_op jit(solution)/shard_map/ppermute | solution.py:20
  139.2 7.2 %collective-permute-start.20 = (f32[3,16,128]{2,1,0:T(8,128)S(1)}, f32[3,16,128]{2,1,0:T(8,128)S(1)}, u32[]{:S(2)}, u32[]{:S(2)}) collective-permute-start(f32[3,16,128]{2,1,0:T(8,128)S(1)} %slice_bitcast_fusion.170), channel_id=1, source_target_pairs={{1,0},{2,1},{3,2},{4,3},{5,4},{6,5},{7,6},{8,7},{9,8},{10,9},{11,1... | collective-permute-start | bytes 73736 | tf_op jit(solution)/shard_map/ppermute | solution.py:20
  146.9 8.8 %collective-permute-start.22 = (f32[3,16,128]{2,1,0:T(8,128)S(1)}, f32[3,16,128]{2,1,0:T(8,128)S(1)}, u32[]{:S(2)}, u32[]{:S(2)}) collective-permute-start(f32[3,16,128]{2,1,0:T(8,128)S(1)} %slice_bitcast_fusion.169), channel_id=1, source_target_pairs={{0,1},{1,2},{2,3},{3,4},{4,5},{5,6},{6,7},{7,8},{8,9},{9,10},{10,1... | collective-permute-start | bytes 73736 | tf_op jit(solution)/shard_map/ppermute | solution.py:20
  148.9 6.8 %collective-permute-start.23 = (f32[3,16,128]{2,0,1:T(4,128)S(1)}, f32[3,16,128]{2,0,1:T(4,128)S(1)}, u32[]{:S(2)}, u32[]{:S(2)}) collective-permute-start(f32[3,16,128]{2,0,1:T(4,128)S(1)} %bitcast.1308), channel_id=1, source_target_pairs={{0,16},{16,32},{32,48},{48,64},{64,80},{80,96},{96,112},{112,128},... | collective-permute-start | bytes 73736 | tf_op jit(solution)/shard_map/ppermute | solution.py:20
  156.2 9.7 %collective-permute-start.25 = (f32[3,16,128]{2,1,0:T(8,128)S(1)}, f32[3,16,128]{2,1,0:T(8,128)S(1)}, u32[]{:S(2)}, u32[]{:S(2)}) collective-permute-start(f32[3,16,128]{2,1,0:T(8,128)S(1)} %bitcast.1338), channel_id=1, source_target_pairs={{16,0},{32,16},{48,32},{64,48},{80,64},{96,80},{112,96},{128,112},... | collective-permute-start | bytes 73736 | tf_op jit(solution)/shard_map/ppermute | solution.py:20
  158.7 8.1 %collective-permute-start.24 = (f32[3,16,128]{2,1,0:T(8,128)S(1)}, f32[3,16,128]{2,1,0:T(8,128)S(1)}, u32[]{:S(2)}, u32[]{:S(2)}) collective-permute-start(f32[3,16,128]{2,1,0:T(8,128)S(1)} %slice_bitcast_fusion.168), channel_id=1, source_target_pairs={{1,0},{2,1},{3,2},{4,3},{5,4},{6,5},{7,6},{8,7},{9,8},{10,9},{11,1... | collective-permute-start | bytes 73736 | tf_op jit(solution)/shard_map/ppermute | solution.py:20
  167.3 8.5 %collective-permute-start.26 = (f32[3,16,128]{2,1,0:T(8,128)S(1)}, f32[3,16,128]{2,1,0:T(8,128)S(1)}, u32[]{:S(2)}, u32[]{:S(2)}) collective-permute-start(f32[3,16,128]{2,1,0:T(8,128)S(1)} %slice_bitcast_fusion.167), channel_id=1, source_target_pairs={{0,1},{1,2},{2,3},{3,4},{4,5},{5,6},{6,7},{7,8},{8,9},{9,10},{10,1... | collective-permute-start | bytes 73736 | tf_op jit(solution)/shard_map/ppermute | solution.py:20
  169.3 6.5 %collective-permute-start.27 = (f32[3,16,128]{2,0,1:T(4,128)S(1)}, f32[3,16,128]{2,0,1:T(4,128)S(1)}, u32[]{:S(2)}, u32[]{:S(2)}) collective-permute-start(f32[3,16,128]{2,0,1:T(4,128)S(1)} %bitcast.1309), channel_id=1, source_target_pairs={{0,16},{16,32},{32,48},{48,64},{64,80},{80,96},{96,112},{112,128},... | collective-permute-start | bytes 73736 | tf_op jit(solution)/shard_map/ppermute | solution.py:20
  176.2 10.0 %collective-permute-start.29 = (f32[3,16,128]{2,1,0:T(8,128)S(1)}, f32[3,16,128]{2,1,0:T(8,128)S(1)}, u32[]{:S(2)}, u32[]{:S(2)}) collective-permute-start(f32[3,16,128]{2,1,0:T(8,128)S(1)} %bitcast.1339), channel_id=1, source_target_pairs={{16,0},{32,16},{48,32},{64,48},{80,64},{96,80},{112,96},{128,112},... | collective-permute-start | bytes 73736 | tf_op jit(solution)/shard_map/ppermute | solution.py:20
  178.2 9.0 %collective-permute-start.28 = (f32[3,16,128]{2,1,0:T(8,128)S(1)}, f32[3,16,128]{2,1,0:T(8,128)S(1)}, u32[]{:S(2)}, u32[]{:S(2)}) collective-permute-start(f32[3,16,128]{2,1,0:T(8,128)S(1)} %slice_bitcast_fusion.166), channel_id=1, source_target_pairs={{1,0},{2,1},{3,2},{4,3},{5,4},{6,5},{7,6},{8,7},{9,8},{10,9},{11,1... | collective-permute-start | bytes 73736 | tf_op jit(solution)/shard_map/ppermute | solution.py:20
  187.8 7.4 %collective-permute-start.31 = (f32[3,16,128]{2,1,0:T(8,128)S(1)}, f32[3,16,128]{2,1,0:T(8,128)S(1)}, u32[]{:S(2)}, u32[]{:S(2)}) collective-permute-start(f32[3,16,128]{2,1,0:T(8,128)S(1)} %bitcast.1329), channel_id=1, source_target_pairs={{0,16},{16,32},{32,48},{48,64},{64,80},{80,96},{96,112},{112,128},... | collective-permute-start | bytes 73736 | tf_op jit(solution)/shard_map/ppermute | solution.py:20
  193.2 9.4 %collective-permute-start.30 = (f32[3,16,128]{2,1,0:T(8,128)S(1)}, f32[3,16,128]{2,1,0:T(8,128)S(1)}, u32[]{:S(2)}, u32[]{:S(2)}) collective-permute-start(f32[3,16,128]{2,1,0:T(8,128)S(1)} %slice_bitcast_fusion.165), channel_id=1, source_target_pairs={{0,1},{1,2},{2,3},{3,4},{4,5},{5,6},{6,7},{7,8},{8,9},{9,10},{10,1... | collective-permute-start | bytes 73736 | tf_op jit(solution)/shard_map/ppermute | solution.py:20
  204.1 5.4 %collective-permute-start.34 = (f32[3,16,128]{2,1,0:T(8,128)S(1)}, f32[3,16,128]{2,1,0:T(8,128)S(1)}, u32[]{:S(2)}, u32[]{:S(2)}) collective-permute-start(f32[3,16,128]{2,1,0:T(8,128)S(1)} %slice_bitcast_fusion.163), channel_id=1, source_target_pairs={{1,0},{2,1},{3,2},{4,3},{5,4},{6,5},{7,6},{8,7},{9,8},{10,9},{11,1... | collective-permute-start | bytes 73736 | tf_op jit(solution)/shard_map/ppermute | solution.py:20
  207.5 6.1 %collective-permute-start.35 = (f32[3,16,128]{2,0,1:T(4,128)S(1)}, f32[3,16,128]{2,0,1:T(4,128)S(1)}, u32[]{:S(2)}, u32[]{:S(2)}) collective-permute-start(f32[3,16,128]{2,0,1:T(4,128)S(1)} %bitcast.1310), channel_id=1, source_target_pairs={{16,0},{32,16},{48,32},{64,48},{80,64},{96,80},{112,96},{128,112},... | collective-permute-start | bytes 73736 | tf_op jit(solution)/shard_map/ppermute | solution.py:20
  214.1 3.9 %collective-permute-start.37 = (f32[3,16,128]{2,0,1:T(4,128)S(1)}, f32[3,16,128]{2,0,1:T(4,128)S(1)}, u32[]{:S(2)}, u32[]{:S(2)}) collective-permute-start(f32[3,16,128]{2,0,1:T(4,128)S(1)} %bitcast.1311), channel_id=1, source_target_pairs={{0,16},{16,32},{32,48},{48,64},{64,80},{80,96},{96,112},{112,128},... | collective-permute-start | bytes 73736 | tf_op jit(solution)/shard_map/ppermute | solution.py:20
  216.1 8.2 %collective-permute-start.36 = (f32[3,16,128]{2,1,0:T(8,128)S(1)}, f32[3,16,128]{2,1,0:T(8,128)S(1)}, u32[]{:S(2)}, u32[]{:S(2)}) collective-permute-start(f32[3,16,128]{2,1,0:T(8,128)S(1)} %slice_bitcast_fusion.162), channel_id=1, source_target_pairs={{0,1},{1,2},{2,3},{3,4},{4,5},{5,6},{6,7},{7,8},{8,9},{9,10},{10,1... | collective-permute-start | bytes 73736 | tf_op jit(solution)/shard_map/ppermute | solution.py:20
  224.7 6.1 %collective-permute-start.39 = (f32[3,16,128]{2,0,1:T(4,128)S(1)}, f32[3,16,128]{2,0,1:T(4,128)S(1)}, u32[]{:S(2)}, u32[]{:S(2)}) collective-permute-start(f32[3,16,128]{2,0,1:T(4,128)S(1)} %bitcast.1312), channel_id=1, source_target_pairs={{16,0},{32,16},{48,32},{64,48},{80,64},{96,80},{112,96},{128,112},... | collective-permute-start | bytes 73736 | tf_op jit(solution)/shard_map/ppermute | solution.py:20
  228.3 4.6 %collective-permute-start.38 = (f32[3,16,128]{2,1,0:T(8,128)S(1)}, f32[3,16,128]{2,1,0:T(8,128)S(1)}, u32[]{:S(2)}, u32[]{:S(2)}) collective-permute-start(f32[3,16,128]{2,1,0:T(8,128)S(1)} %slice_bitcast_fusion.161), channel_id=1, source_target_pairs={{1,0},{2,1},{3,2},{4,3},{5,4},{6,5},{7,6},{8,7},{9,8},{10,9},{11,1... | collective-permute-start | bytes 73736 | tf_op jit(solution)/shard_map/ppermute | solution.py:20
  233.6 6.1 %collective-permute-start.41 = (f32[3,16,128]{2,0,1:T(4,128)S(1)}, f32[3,16,128]{2,0,1:T(4,128)S(1)}, u32[]{:S(2)}, u32[]{:S(2)}) collective-permute-start(f32[3,16,128]{2,0,1:T(4,128)S(1)} %bitcast.1302), channel_id=1, source_target_pairs={{0,16},{16,32},{32,48},{48,64},{64,80},{80,96},{96,112},{112,128},... | collective-permute-start | bytes 73736 | tf_op jit(solution)/shard_map/ppermute | solution.py:20
  237.7 8.2 %collective-permute-start.40 = (f32[3,16,128]{2,1,0:T(8,128)S(1)}, f32[3,16,128]{2,1,0:T(8,128)S(1)}, u32[]{:S(2)}, u32[]{:S(2)}) collective-permute-start(f32[3,16,128]{2,1,0:T(8,128)S(1)} %slice_bitcast_fusion.160), channel_id=1, source_target_pairs={{0,1},{1,2},{2,3},{3,4},{4,5},{5,6},{6,7},{7,8},{8,9},{9,10},{10,1... | collective-permute-start | bytes 73736 | tf_op jit(solution)/shard_map/ppermute | solution.py:20
  246.5 6.1 %collective-permute-start.43 = (f32[3,16,128]{2,0,1:T(4,128)S(1)}, f32[3,16,128]{2,0,1:T(4,128)S(1)}, u32[]{:S(2)}, u32[]{:S(2)}) collective-permute-start(f32[3,16,128]{2,0,1:T(4,128)S(1)} %bitcast.1313), channel_id=1, source_target_pairs={{16,0},{32,16},{48,32},{64,48},{80,64},{96,80},{112,96},{128,112},... | collective-permute-start | bytes 73736 | tf_op jit(solution)/shard_map/ppermute | solution.py:20
  248.6 4.6 %collective-permute-start.42 = (f32[3,16,128]{2,1,0:T(8,128)S(1)}, f32[3,16,128]{2,1,0:T(8,128)S(1)}, u32[]{:S(2)}, u32[]{:S(2)}) collective-permute-start(f32[3,16,128]{2,1,0:T(8,128)S(1)} %slice_bitcast_fusion.159), channel_id=1, source_target_pairs={{1,0},{2,1},{3,2},{4,3},{5,4},{6,5},{7,6},{8,7},{9,8},{10,9},{11,1... | collective-permute-start | bytes 73736 | tf_op jit(solution)/shard_map/ppermute | solution.py:20
  253.7 7.5 %collective-permute-start.45 = (f32[3,16,128]{2,1,0:T(8,128)S(1)}, f32[3,16,128]{2,1,0:T(8,128)S(1)}, u32[]{:S(2)}, u32[]{:S(2)}) collective-permute-start(f32[3,16,128]{2,1,0:T(8,128)S(1)} %bitcast.1330), channel_id=1, source_target_pairs={{0,16},{16,32},{32,48},{48,64},{64,80},{80,96},{96,112},{112,128},... | collective-permute-start | bytes 73736 | tf_op jit(solution)/shard_map/ppermute | solution.py:20
  259.2 8.2 %collective-permute-start.44 = (f32[3,16,128]{2,1,0:T(8,128)S(1)}, f32[3,16,128]{2,1,0:T(8,128)S(1)}, u32[]{:S(2)}, u32[]{:S(2)}) collective-permute-start(f32[3,16,128]{2,1,0:T(8,128)S(1)} %slice_bitcast_fusion.158), channel_id=1, source_target_pairs={{0,1},{1,2},{2,3},{3,4},{4,5},{5,6},{6,7},{7,8},{8,9},{9,10},{10,1... | collective-permute-start | bytes 73736 | tf_op jit(solution)/shard_map/ppermute | solution.py:20
  267.9 6.1 %collective-permute-start.47 = (f32[3,16,128]{2,0,1:T(4,128)S(1)}, f32[3,16,128]{2,0,1:T(4,128)S(1)}, u32[]{:S(2)}, u32[]{:S(2)}) collective-permute-start(f32[3,16,128]{2,0,1:T(4,128)S(1)} %bitcast.1314), channel_id=1, source_target_pairs={{16,0},{32,16},{48,32},{64,48},{80,64},{96,80},{112,96},{128,112},... | collective-permute-start | bytes 73736 | tf_op jit(solution)/shard_map/ppermute | solution.py:20
  269.8 4.6 %collective-permute-start.46 = (f32[3,16,128]{2,1,0:T(8,128)S(1)}, f32[3,16,128]{2,1,0:T(8,128)S(1)}, u32[]{:S(2)}, u32[]{:S(2)}) collective-permute-start(f32[3,16,128]{2,1,0:T(8,128)S(1)} %slice_bitcast_fusion.157), channel_id=1, source_target_pairs={{1,0},{2,1},{3,2},{4,3},{5,4},{6,5},{7,6},{8,7},{9,8},{10,9},{11,1... | collective-permute-start | bytes 73736 | tf_op jit(solution)/shard_map/ppermute | solution.py:20
  275.0 7.7 %collective-permute-start.49 = (f32[3,16,128]{2,0,1:T(4,128)S(1)}, f32[3,16,128]{2,0,1:T(4,128)S(1)}, u32[]{:S(2)}, u32[]{:S(2)}) collective-permute-start(f32[3,16,128]{2,0,1:T(4,128)S(1)} %bitcast.1301), channel_id=1, source_target_pairs={{0,16},{16,32},{32,48},{48,64},{64,80},{80,96},{96,112},{112,128},... | collective-permute-start | bytes 73736 | tf_op jit(solution)/shard_map/ppermute | solution.py:20
  280.7 8.2 %collective-permute-start.48 = (f32[3,16,128]{2,1,0:T(8,128)S(1)}, f32[3,16,128]{2,1,0:T(8,128)S(1)}, u32[]{:S(2)}, u32[]{:S(2)}) collective-permute-start(f32[3,16,128]{2,1,0:T(8,128)S(1)} %slice_bitcast_fusion.156), channel_id=1, source_target_pairs={{0,1},{1,2},{2,3},{3,4},{4,5},{5,6},{6,7},{7,8},{8,9},{9,10},{10,1... | collective-permute-start | bytes 73736 | tf_op jit(solution)/shard_map/ppermute | solution.py:20
  289.4 6.1 %collective-permute-start.51 = (f32[3,16,128]{2,0,1:T(4,128)S(1)}, f32[3,16,128]{2,0,1:T(4,128)S(1)}, u32[]{:S(2)}, u32[]{:S(2)}) collective-permute-start(f32[3,16,128]{2,0,1:T(4,128)S(1)} %bitcast.1315), channel_id=1, source_target_pairs={{16,0},{32,16},{48,32},{64,48},{80,64},{96,80},{112,96},{128,112},... | collective-permute-start | bytes 73736 | tf_op jit(solution)/shard_map/ppermute | solution.py:20
  291.4 4.6 %collective-permute-start.50 = (f32[3,16,128]{2,1,0:T(8,128)S(1)}, f32[3,16,128]{2,1,0:T(8,128)S(1)}, u32[]{:S(2)}, u32[]{:S(2)}) collective-permute-start(f32[3,16,128]{2,1,0:T(8,128)S(1)} %slice_bitcast_fusion.155), channel_id=1, source_target_pairs={{1,0},{2,1},{3,2},{4,3},{5,4},{6,5},{7,6},{8,7},{9,8},{10,9},{11,1... | collective-permute-start | bytes 73736 | tf_op jit(solution)/shard_map/ppermute | solution.py:20
  296.3 7.7 %collective-permute-start.53 = (f32[3,16,128]{2,1,0:T(8,128)S(1)}, f32[3,16,128]{2,1,0:T(8,128)S(1)}, u32[]{:S(2)}, u32[]{:S(2)}) collective-permute-start(f32[3,16,128]{2,1,0:T(8,128)S(1)} %bitcast.1331), channel_id=1, source_target_pairs={{0,16},{16,32},{32,48},{48,64},{64,80},{80,96},{96,112},{112,128},... | collective-permute-start | bytes 73736 | tf_op jit(solution)/shard_map/ppermute | solution.py:20
  302.1 8.2 %collective-permute-start.52 = (f32[3,16,128]{2,1,0:T(8,128)S(1)}, f32[3,16,128]{2,1,0:T(8,128)S(1)}, u32[]{:S(2)}, u32[]{:S(2)}) collective-permute-start(f32[3,16,128]{2,1,0:T(8,128)S(1)} %slice_bitcast_fusion.154), channel_id=1, source_target_pairs={{0,1},{1,2},{2,3},{3,4},{4,5},{5,6},{6,7},{7,8},{8,9},{9,10},{10,1... | collective-permute-start | bytes 73736 | tf_op jit(solution)/shard_map/ppermute | solution.py:20
  310.8 6.1 %collective-permute-start.55 = (f32[3,16,128]{2,0,1:T(4,128)S(1)}, f32[3,16,128]{2,0,1:T(4,128)S(1)}, u32[]{:S(2)}, u32[]{:S(2)}) collective-permute-start(f32[3,16,128]{2,0,1:T(4,128)S(1)} %bitcast.1316), channel_id=1, source_target_pairs={{16,0},{32,16},{48,32},{64,48},{80,64},{96,80},{112,96},{128,112},... | collective-permute-start | bytes 73736 | tf_op jit(solution)/shard_map/ppermute | solution.py:20
  312.8 4.6 %collective-permute-start.54 = (f32[3,16,128]{2,1,0:T(8,128)S(1)}, f32[3,16,128]{2,1,0:T(8,128)S(1)}, u32[]{:S(2)}, u32[]{:S(2)}) collective-permute-start(f32[3,16,128]{2,1,0:T(8,128)S(1)} %slice_bitcast_fusion.153), channel_id=1, source_target_pairs={{1,0},{2,1},{3,2},{4,3},{5,4},{6,5},{7,6},{8,7},{9,8},{10,9},{11,1... | collective-permute-start | bytes 73736 | tf_op jit(solution)/shard_map/ppermute | solution.py:20
  317.9 8.2 %collective-permute-start.56 = (f32[3,16,128]{2,1,0:T(8,128)S(1)}, f32[3,16,128]{2,1,0:T(8,128)S(1)}, u32[]{:S(2)}, u32[]{:S(2)}) collective-permute-start(f32[3,16,128]{2,1,0:T(8,128)S(1)} %bitcast.1333), channel_id=1, source_target_pairs={{0,1},{1,2},{2,3},{3,4},{4,5},{5,6},{6,7},{7,8},{8,9},{9,10},{10,1... | collective-permute-start | bytes 73736 | tf_op jit(solution)/shard_map/ppermute | solution.py:20
  319.9 6.6 %collective-permute-start.57 = (f32[3,16,128]{2,1,0:T(8,128)S(1)}, f32[3,16,128]{2,1,0:T(8,128)S(1)}, u32[]{:S(2)}, u32[]{:S(2)}) collective-permute-start(f32[3,16,128]{2,1,0:T(8,128)S(1)} %slice_bitcast_fusion.152), channel_id=1, source_target_pairs={{0,16},{16,32},{32,48},{48,64},{64,80},{80,96},{96,112},{112,128},... | collective-permute-start | bytes 73736 | tf_op jit(solution)/shard_map/ppermute | solution.py:20
  327.1 13.6 %collective-permute-start.58 = (f32[3,16,128]{2,1,0:T(8,128)S(1)}, f32[3,16,128]{2,1,0:T(8,128)S(1)}, u32[]{:S(2)}, u32[]{:S(2)}) collective-permute-start(f32[3,16,128]{2,1,0:T(8,128)S(1)} %bitcast.1327), channel_id=1, source_target_pairs={{1,0},{2,1},{3,2},{4,3},{5,4},{6,5},{7,6},{8,7},{9,8},{10,9},{11,1... | collective-permute-start | bytes 73736 | tf_op jit(solution)/shard_map/ppermute | solution.py:20
  334.9 6.3 %collective-permute-start.59 = (f32[3,16,128]{2,1,0:T(8,128)S(1)}, f32[3,16,128]{2,1,0:T(8,128)S(1)}, u32[]{:S(2)}, u32[]{:S(2)}) collective-permute-start(f32[3,16,128]{2,1,0:T(8,128)S(1)} %slice_bitcast_fusion.151), channel_id=1, source_target_pairs={{16,0},{32,16},{48,32},{64,48},{80,64},{96,80},{112,96},{128,112},... | collective-permute-start | bytes 73736 | tf_op jit(solution)/shard_map/ppermute | solution.py:20
  341.7 8.2 %collective-permute-start.60 = (f32[3,16,128]{2,1,0:T(8,128)S(1)}, f32[3,16,128]{2,1,0:T(8,128)S(1)}, u32[]{:S(2)}, u32[]{:S(2)}) collective-permute-start(f32[3,16,128]{2,1,0:T(8,128)S(1)} %bitcast.1334), channel_id=1, source_target_pairs={{0,1},{1,2},{2,3},{3,4},{4,5},{5,6},{6,7},{7,8},{8,9},{9,10},{10,1... | collective-permute-start | bytes 73736 | tf_op jit(solution)/shard_map/ppermute | solution.py:20
  343.7 6.3 %collective-permute-start.61 = (f32[3,16,128]{2,1,0:T(8,128)S(1)}, f32[3,16,128]{2,1,0:T(8,128)S(1)}, u32[]{:S(2)}, u32[]{:S(2)}) collective-permute-start(f32[3,16,128]{2,1,0:T(8,128)S(1)} %slice_bitcast_fusion.150), channel_id=1, source_target_pairs={{0,16},{16,32},{32,48},{48,64},{64,80},{80,96},{96,112},{112,128},... | collective-permute-start | bytes 73736 | tf_op jit(solution)/shard_map/ppermute | solution.py:20
  350.3 8.8 %collective-permute-start.62 = (f32[3,16,128]{2,1,0:T(8,128)S(1)}, f32[3,16,128]{2,1,0:T(8,128)S(1)}, u32[]{:S(2)}, u32[]{:S(2)}) collective-permute-start(f32[3,16,128]{2,1,0:T(8,128)S(1)} %bitcast.1332), channel_id=1, source_target_pairs={{1,0},{2,1},{3,2},{4,3},{5,4},{6,5},{7,6},{8,7},{9,8},{10,9},{11,1... | collective-permute-start | bytes 73736 | tf_op jit(solution)/shard_map/ppermute | solution.py:20
  357.2 6.3 %collective-permute-start.63 = (f32[3,16,128]{2,1,0:T(8,128)S(1)}, f32[3,16,128]{2,1,0:T(8,128)S(1)}, u32[]{:S(2)}, u32[]{:S(2)}) collective-permute-start(f32[3,16,128]{2,1,0:T(8,128)S(1)} %slice_bitcast_fusion.149), channel_id=1, source_target_pairs={{16,0},{32,16},{48,32},{64,48},{80,64},{96,80},{112,96},{128,112},... | collective-permute-start | bytes 73736 | tf_op jit(solution)/shard_map/ppermute | solution.py:20
  (10 other events, 31.3 us)
where the time goes:
time: 367 us; the launch traced here: 365 us
  starting transfers between devices  222 us (60%)
  waiting for transfers between devices  88.2 us (24%)
  other arithmetic  19.3 us (5%)
  blocking collectives  15.8 us (4%)
  local copies, waits for them, and re-layouts  14.8 us (4%)
  between operations  3.84 us (1%)
    ppermute x64, starting transfers between devices, shifted(): lax.ppermute(value, axis, [(source, source + steps) for source in range(l...  222 us
    ppermute x64, waiting for transfers between devices, shifted(): lax.ppermute(value, axis, [(source, source + steps) for source in range(l...  88.2 us
    all_gather x1, blocking collectives, carried_in(): pieces = lax.all_gather(value, axis)  15.8 us
  transfers between devices with their start and end apart: 64, of which 36 were waited for; matrix products, arithmetic and copies ran while one was open for 4% of the time, Pallas kernels for 0%

commit v1 on v0

v1 whole, which is shorter than its diff:
```python
import functools
import math

import jax
import jax.numpy as jnp
import numpy as np
from jax import lax
from jax.experimental import pallas as pl
from jax.experimental.pallas import tpu as pltpu
from jax.sharding import PartitionSpec as P

STEPS = 8
FIRST = 3
SECOND = STEPS - FIRST
DOM = 8
BINS = 8
OMEGA = 0.9
CELLS = 16
LANES = 128
CHIP = 2 * CELLS

XO, XN, YO, YN = -12, 40, -12, 48
XA, XAN, YA, YAN = -8, 32, -8, 40
YF, YFN = -4, 26

CURL_E = (
    (0, 2, 0, 0), (0, 2, 0, 1), (0, 1, 0, 0),
    (1, 0, 0, 0), (1, 2, 0, 0), (1, 2, 1, 0),
    (2, 1, 0, 0), (2, 1, 1, 0), (2, 0, 0, 0), (2, 0, 0, 1),
)
CURL_H = tuple((o, i, -dx, -dy) for o, i, dx, dy in CURL_E)

MARGIN = 16
SPAN = CELLS + 2 * MARGIN


def own_cells():
    cells = np.zeros((3, SPAN, SPAN), bool)
    cells[:, MARGIN : MARGIN + CELLS, MARGIN : MARGIN + CELLS] = True
    return cells


def reads(target, source, stencil):
    for result, read, dx, dy in stencil:
        target[read] |= np.roll(source[result], (dx, dy), (0, 1))


def box(cells):
    flat = cells.any(0) if cells.ndim == 3 else cells
    xs, ys = (np.flatnonzero(flat.any(1)), np.flatnonzero(flat.any(0)))
    return (int(xs[0]) - MARGIN, int(xs[-1]) + 1 - MARGIN, int(ys[0]) - MARGIN, int(ys[-1]) + 1 - MARGIN)


def adjoint_needs(steps):
    need_e, need_h = own_cells(), own_cells()
    coef = np.zeros((SPAN, SPAN), bool)
    source, box_e, box_h = {}, {}, {}
    for left in range(1, steps + 1):
        box_h[left] = box(need_h)
        electric = need_e.copy()
        reads(electric, need_h, CURL_E)
        before = need_h.copy()
        reads(before, electric, CURL_H)
        coef |= electric.any(0)
        source[left], box_e[left] = electric, box(electric)
        need_e, need_h = electric, before
    return need_e, need_h, coef, source, box_e, box_h


ADJ1 = adjoint_needs(FIRST)
ADJ2 = adjoint_needs(SECOND)


def forward_needs():
    wanted = {n: ADJ2[3][n] for n in range(1, SECOND + 1)}
    wanted.update({n + SECOND: ADJ1[3][n] for n in range(1, FIRST + 1)})
    electric, magnetic = np.zeros((3, SPAN, SPAN), bool), np.zeros((3, SPAN, SPAN), bool)
    coef = ADJ1[2] | ADJ2[2]
    box_e, box_h = {}, {}
    for n in range(STEPS, 0, -1):
        electric |= wanted[n]
        box_e[n] = box(electric)
        coef |= electric.any(0)
        reads(magnetic, electric, CURL_H)
        box_h[n] = box(magnetic)
        reads(electric, magnetic, CURL_E)
    return electric, magnetic, coef, box_e, box_h, {n: box(wanted[n]) for n in wanted}


FWD = forward_needs()


def spans(cells):
    found = {}
    for column in range(SPAN):
        xs = np.flatnonzero(cells[:, column])
        if xs.size:
            found[column - MARGIN] = (int(xs[0]) - MARGIN, int(xs[-1]) + 1 - MARGIN)
    return found


NEEDS1 = [spans(c) for c in (*FWD[0], *FWD[1], FWD[2], *ADJ1[0], *ADJ1[1])]
NEEDS2 = [spans(c) for c in (*ADJ2[0], *ADJ2[1])]


class Message:
    def __init__(self, wanted):
        self.at, rows = {}, 0
        for key in sorted(wanted):
            first, last = wanted[key]
            if last > first:
                self.at[key] = (first, last, rows)
                rows += last - first
        self.rows = rows


class Exchange:
    def __init__(self, needs):
        a0, a1, b0, b1, cr1, cl1, cr2, cl2 = ({} for _ in range(8))
        for f, columns in enumerate(needs):
            for y, (x0, x1) in columns.items():
                if 0 <= y < CELLS:
                    a0[f, y] = (x0, min(x1, 0))
                    a1[f, y] = (CHIP, CELLS + x1)
                    b0[f, y] = (CELLS, x1)
                    b1[f, y] = (CELLS + x0, CELLS)
        for f, columns in enumerate(needs):
            for y, (x0, x1) in columns.items():
                if 0 <= y < CELLS:
                    continue
                first, last = (x0, x1 + CELLS)
                one, two = (cr1, cr2) if y < 0 else (cl1, cl2)
                one[f, y] = (max(first, 0), min(last, CHIP))
                two[f, y, -1] = (first, min(last, 0))
                two[f, y, 1] = (max(first, CHIP), last)
                if y < 0:
                    b0[f, y + CELLS] = (CELLS, max(b0.get((f, y + CELLS), (0, CELLS))[1], min(last, CHIP)))
                else:
                    b1[f, y - CELLS] = (min(b1.get((f, y - CELLS), (CELLS, 0))[0], max(first, 0)), CELLS)
        self.a = (Message(a0), Message(a1))
        self.b = (Message(b0), Message(b1))
        self.c1 = (Message(cl1), Message(cr1))
        self.c2 = (Message(cl2), Message(cr2))
        self.rows = {
            name: -(-max(m.rows for m in getattr(self, name)) // 8) * 8 for name in ("a", "b", "c1", "c2")
        }


EX1 = Exchange(NEEDS1)
EX2 = Exchange(NEEDS2)


def take(message, ref, key, first, last):
    x0, x1, row = message.at[key]
    assert x0 <= first and last <= x1
    return ref[row + first - x0 : row + last - x0, :]


def inside(core, exchange, own, refs, f, y, first, last):
    origins = (
        (-MARGIN, 0, exchange.a[0], "a" if core == 0 else "a_other"),
        (0, CELLS, exchange.b[1], "own" if core == 0 else "b"),
        (CELLS, CHIP, exchange.b[0], "b" if core == 0 else "own"),
        (CHIP, CHIP + MARGIN, exchange.a[1], "a_other" if core == 0 else "a"),
    )
    pieces = []
    for low, high, message, name in origins:
        x0, x1 = (max(first, low), min(last, high))
        if x1 > x0:
            if name == "own":
                pieces.append((x0, x1, own[f, y * CELLS + x0 - low : y * CELLS + x1 - low, :]))
            else:
                pieces.append((x0, x1, take(message, refs[name], (f, y), x0, x1)))
    return pieces


def outside(core, exchange, refs, f, y, first, last):
    receiver = 0 if y >= CELLS else 1
    suffix = "" if receiver == core else "_other"
    pieces = []
    for low, high, name, side in ((-MARGIN, 0, "c2", -1), (0, CHIP, "c1", 0), (CHIP, CHIP + MARGIN, "c2", 1)):
        x0, x1 = (max(first, low), min(last, high))
        if x1 > x0:
            key = (f, y, side) if side else (f, y)
            pieces.append((x0, x1, take(getattr(exchange, name)[receiver], refs[name + suffix], key, x0, x1)))
    return pieces


def put(out, row, x_start, pieces):
    for x0, x1, value in pieces:
        out[row + x0 - x_start : row + x1 - x_start, :] = value


def pack_a(core, exchange, own, out):
    shift = (-CHIP if core == 0 else CHIP) - CELLS * core
    for (f, y), (x0, x1, row) in exchange.a[1 - core].at.items():
        out[row : row + x1 - x0, :] = own[f, y * CELLS + x0 + shift : y * CELLS + x1 + shift, :]


def pack_b(core, exchange, own, out):
    for (f, y), (x0, x1, row) in exchange.b[1 - core].at.items():
        at = y * CELLS - CELLS * core
        out[row : row + x1 - x0, :] = own[f, at + x0 : at + x1, :]


def pack_c(core, exchange, own, refs, name, out):
    shift = CELLS if core == 0 else -CELLS
    for key, (x0, x1, row) in getattr(exchange, name)[1 - core].at.items():
        put(out, row, x0, inside(core, exchange, own, refs, key[0], key[1] + shift, x0, x1))


def unpack(core, exchange, needs, own, refs, store):
    base = CELLS * core
    for f, columns in enumerate(needs):
        for y, (x0, x1) in columns.items():
            if 0 <= y < CELLS:
                pieces = inside(core, exchange, own, refs, f, y, x0 + base, x1 + base)
            else:
                pieces = outside(core, exchange, refs, f, y, x0 + base, x1 + base)
            for first, _, value in pieces:
                store(f, y, first - base, value)


def columns_loop(first, last, vregs, body):
    count = last - first
    trips = max(1, round(count * vregs / 110))
    group = -(-count // trips)
    trips = -(-count // group)
    if trips == 1:
        body(0, group)
        return

    def turn(i, carry):
        body(i * group, group)
        return carry

    lax.fori_loop(0, trips, turn, 0)


def rows_of(span, origin, width):
    x0, x1 = span
    count = min(width, -(-(x1 - x0) // 8) * 8)
    return min(x0, origin + width - count) - origin, count


def magnetic_pass(electric, magnetic, sign, bounds, window):
    x0, x1, y0, y1 = bounds
    xo, xn, yo, _ = window
    offset, count = rows_of((x0, x1), xo, xn)

    def body(start, group):
        last = lax.broadcasted_iota(jnp.int32, (count, LANES), 1) == LANES - 1
        for j in range(group):
            row = (start + (j + y0 - yo)) * xn + offset
            here, up_x, up_y = (pl.ds(row + d, count) for d in (0, 1, xn))
            ex, ey, ez = (electric[c, here, :] for c in range(3))
            ey_z = jnp.where(last, 0.0, pltpu.roll(ey, LANES - 1, 1)) - ey
            ex_z = jnp.where(last, 0.0, pltpu.roll(ex, LANES - 1, 1)) - ex
            curl = (
                (electric[2, up_y, :] - ez) - ey_z,
                ex_z - (electric[2, up_x, :] - ez),
                (electric[1, up_x, :] - ey) - (electric[0, up_y, :] - ex),
            )
            for c in range(3):
                magnetic[c, here, :] = magnetic[c, here, :] + curl[c] if sign > 0 else magnetic[c, here, :] - curl[c]

    columns_loop(y0, y1, count // 8, body)


def electric_pass(magnetic, electric, coef, sign, bounds, window):
    x0, x1, y0, y1 = bounds
    xo, xn, yo, _ = window
    offset, count = rows_of((x0, x1), xo, xn)

    def body(start, group):
        first = lax.broadcasted_iota(jnp.int32, (count, LANES), 1) == 0
        for j in range(group):
            row = (start + (j + y0 - yo)) * xn + offset
            here, down_x, down_y = (pl.ds(row - d, count) for d in (0, 1, xn))
            hx, hy, hz = (magnetic[c, here, :] for c in range(3))
            hy_z = hy - jnp.where(first, 0.0, pltpu.roll(hy, 1, 1))
            hx_z = hx - jnp.where(first, 0.0, pltpu.roll(hx, 1, 1))
            curl = (
                (hz - magnetic[2, down_y, :]) - hy_z,
                hx_z - (hz - magnetic[2, down_x, :]),
                (hy - magnetic[1, down_x, :]) - (hx - magnetic[0, down_y, :]),
            )
            scale = coef[here, :]
            for c in range(3):
                change = scale * curl[c]
                electric[c, here, :] = electric[c, here, :] + change if sign > 0 else electric[c, here, :] - change

    columns_loop(y0, y1, count // 8, body)


def clear_outside(ids, magnetic, bounds, window):
    _, _, y0, y1 = bounds
    xo, xn, yo, _ = window

    @pl.when(ids[1] == 0)
    def _():
        zero = jnp.zeros((y1 - y0, LANES), jnp.float32)
        for c in (1, 2):
            magnetic[c, pl.ds((y0 - yo) * xn - 1 - xo, y1 - y0, stride=xn), :] = zero

    if y0 < 0:

        @pl.when(ids[2] == 0)
        def _():
            zero = jnp.zeros((xn, LANES), jnp.float32)
            for c in (0, 2):
                magnetic[c, (-1 - yo) * xn : -yo * xn, :] = zero


def adjoint_steps(ids, numbers, needs, electric, magnetic, coef, kept, drive, sums, sum_row):
    window = (XA, XAN, YA, YAN)
    for done, n in enumerate(numbers):
        left = len(numbers) - done
        bounds = needs[4][left]
        _, _, y0, y1 = bounds
        field = kept(n)
        for y in range(y0, y1):
            factor = drive[n - 1, y // DOM + 1, :, :]
            at, at_kept = ((y - YA) * XAN, (y - YF) * XAN)
            total = None
            for c in range(3):
                value = field[c, at_kept : at_kept + XAN, :]
                new = electric[c, at : at + XAN, :] + factor * value
                electric[c, at : at + XAN, :] = new
                term = new * value
                total = term if total is None else total + term
            if 0 <= y < CELLS:
                slot = sum_row(n) + (y // DOM) * CELLS
                part = total[-XA : CELLS - XA, :]
                if y % DOM == 0:
                    acc = part
                else:
                    acc = acc + part
                if y % DOM == DOM - 1:
                    sums[slot : slot + CELLS, :] = acc
        electric_pass(magnetic, electric, coef, -1, bounds, window)
        after = needs[5][left]
        magnetic_pass(electric, magnetic, 1, after, window)
        clear_outside(ids, magnetic, after, window)


def both_cores(ids, work):
    for core in (0, 1):

        @pl.when(ids[0] == core)
        def _(core=core):
            work(core)


def kernel_start(ids, poling, e, h, m, ae, ah, own, out_a, out_b, sent, raw, raw_m, arrived):
    loads = [(e, raw.at[0:3]), (h, raw.at[3:6]), (m, raw_m), (ae, raw.at[6:9]), (ah, raw.at[9:12])]
    copies = [pltpu.make_async_copy(source, to, arrived.at[k]) for k, (source, to) in enumerate(loads)]
    for copy in copies:
        copy.start()
    lane = lax.broadcasted_iota(jnp.int32, (8, LANES), 1)
    domain = lane % 32 - 2 * ids[1]
    second = (lane // 32) % 2 == 1
    sign = [jnp.where(second, 2 * poling[d, 1] - 1, 2 * poling[d, 0] - 1).astype(jnp.float32) for d in range(2)]
    before = jnp.where(domain > 0, sign[0], 0.0) - jnp.where(domain > 1, sign[1], 0.0)
    here = jnp.where(domain == 0, sign[0], 0.0) + jnp.where(domain == 1, sign[1], 0.0)
    mine = jnp.where(lane < 64, before, here)
    for k in range(sent.shape[0]):
        sent[k, :, :] = mine
    for k, (first, count) in enumerate(((0, 3), (3, 3), (6, 1), (7, 3), (10, 3))):
        copies[k].wait()
        for f in range(first, first + count):
            for y in range(CELLS):
                rows = pl.ds(y, CELLS, stride=CELLS)
                value = raw_m[rows, :].astype(jnp.float32) + 1.0 if f == 6 else raw[f if f < 6 else f - 1, rows, :]
                own[f, y * CELLS : (y + 1) * CELLS, :] = value

    def work(core):
        pack_a(core, EX1, own, out_a)
        pack_b(core, EX1, own, out_b)

    both_cores(ids, work)


def kernel_c1(exchange, ids, own, b, out):
    both_cores(ids, lambda core: pack_c(core, exchange, own, {"b": b}, "c1", out))


def kernel_c2(exchange, ids, own, a, a_other, *rest):
    out = rest[-1]
    both_cores(ids, lambda core: pack_c(core, exchange, own, {"a": a, "a_other": a_other}, "c2", out))
    if len(rest) == 2:
        rows = exchange.rows["c2"]
        out[rows : rows + 8, :] = rest[0][...]


def drive_tables(ids, env_left, env, env_right, beta, alpha, drive):
    lane = lax.broadcasted_iota(jnp.int32, (8, LANES), 1)
    rows = ((env_left, 1), (env, 0), (env, 1), (env_right, 0))
    for w, (row, which) in enumerate(rows):
        for d in range(4):
            index = jnp.clip(2 * ids[1] + d - 1, 0, 31)
            prefix = jnp.sum(jnp.where(lane == index + 32 * which, row, 0.0), axis=1, keepdims=True)
            sign = jnp.sum(jnp.where(lane == index + 32 * which + 64, row, 0.0), axis=1, keepdims=True)
            prefix = jnp.broadcast_to(prefix, (8, LANES))
            sign = jnp.broadcast_to(sign if d % 2 else -sign, (8, LANES))
            for n in range(STEPS):
                drive[n, w, d * DOM : (d + 1) * DOM, :] = prefix * alpha[n] + sign * beta[n, :, :]


NAMES = ("a", "a_other", "b", "c1", "c1_other", "c2", "c2_other")


def kernel_first(alpha, ids, perm, own, *rest):
    refs = dict(zip(NAMES, rest))
    (env, beta, out_a, out_b, own2, coef_a, kept, sums, drive, ef, hf, mf, coef, ea, ga, late, chi) = rest[len(NAMES) :]

    def store(f, y, x, value):
        count = value.shape[0]
        if f <= 6:
            row = (y - YO) * XN + x - XO
            if f < 3:
                ef[f, row : row + count, :] = value
            elif f < 6:
                hf[f - 3, row : row + count, :] = 2.0 * value
            else:
                mf[row : row + count, :] = value
        else:
            row = (y - YA) * XAN + x - XA
            if f < 10:
                ea[f - 7, row : row + count, :] = value
            else:
                ga[f - 10, row : row + count, :] = 2.0 * value

    both_cores(ids, lambda core: unpack(core, EX1, NEEDS1, own, refs, store))
    env_c, env_d = (refs[k][EX1.rows["c2"] : EX1.rows["c2"] + 8, :] for k in ("c2", "c2_other"))
    left = jnp.where(ids[0] == 0, env_d, env_c)
    right = jnp.where(ids[0] == 0, env_c, env_d)
    drive_tables(ids, left, env[...], right, beta, alpha, drive)

    def coefficients(start, group):
        for j in range(group):
            rows = pl.ds((start + j) * XN, XN)
            index = mf[rows, :]
            value = jnp.zeros((XN, LANES), jnp.float32)
            for k in range(4):
                value = jnp.where(index == float(k + 1), 0.25 * perm[k], value)
            coef[rows, :] = value

    columns_loop(0, YN, XN // 8, coefficients)
    for y in range(YF, YF + YFN):
        at = (y - YO) * XN + XA - XO
        chi[(y - YF) * XAN : (y - YF + 1) * XAN, :] = (mf[at : at + XAN, :] == 1.0).astype(jnp.float32)
    for y in range(YA, YA + 32):
        at = (y - YO) * XN + XA - XO
        coef_a[(y - YA) * XAN : (y - YA + 1) * XAN, :] = coef[at : at + XAN, :]

    window = (XO, XN, YO, YN)
    for n in range(1, STEPS + 1):
        magnetic_pass(ef, hf, -1, FWD[4][n], window)
        clear_outside(ids, hf, FWD[4][n], window)
        electric_pass(hf, ef, coef, 1, FWD[3][n], window)
        _, _, y0, y1 = FWD[5][n]
        target = kept.at[n - 1] if n <= SECOND else late.at[n - 1 - SECOND]

        def keep(start, group, y0=y0, target=target):
            for j in range(group):
                rows = pl.ds((start + (j + y0 - YO)) * XN + XA - XO, XAN)
                to = pl.ds((start + (j + y0 - YF)) * XAN, XAN)
                mask = chi[to, :]
                for k in range(3):
                    target[k, to, :] = ef[k, rows, :] * mask

        for y in range(0, y1 - y0):
            keep(y, 1)

    adjoint_steps(ids, list(range(STEPS, SECOND, -1)), ADJ1, ea, ga, coef_a, lambda n: late.at[n - 1 - SECOND], drive, sums,
                  lambda n: (n - 1 - SECOND) * 2 * CELLS)
    for y in range(CELLS):
        at = (y - YA) * XAN - XA
        for k in range(3):
            own2[k, y * CELLS : (y + 1) * CELLS, :] = ea[k, at : at + CELLS, :]
            own2[k + 3, y * CELLS : (y + 1) * CELLS, :] = ga[k, at : at + CELLS, :]

    def work(core):
        pack_a(core, EX2, own2, out_a)
        pack_b(core, EX2, own2, out_b)

    both_cores(ids, work)


def kernel_second(ids, own, *rest):
    refs = dict(zip(NAMES, rest))
    coef_a, kept, sums1, drive, waves, out_e, out_h, out_g, ea, ga, sums2 = rest[len(NAMES) :]

    def store(f, y, x, value):
        row = (y - YA) * XAN + x - XA
        (ea if f < 3 else ga)[f % 3, row : row + value.shape[0], :] = value

    both_cores(ids, lambda core: unpack(core, EX2, NEEDS2, own, refs, store))
    adjoint_steps(ids, list(range(SECOND, 0, -1)), ADJ2, ea, ga, coef_a, lambda n: kept.at[n - 1], drive, sums2,
                  lambda n: (n - 1) * 2 * CELLS)
    for x in range(CELLS):
        for k in range(3):
            rows = pl.ds(-YA * XAN + x - XA, CELLS, stride=XAN)
            out_e[k, x * CELLS : (x + 1) * CELLS, :] = ea[k, rows, :]
            out_h[k, x * CELLS : (x + 1) * CELLS, :] = 0.5 * ga[k, rows, :]
    total = {(x, w): jnp.zeros((2, BINS), jnp.float32) for x in range(2) for w in range(2)}
    for n in range(1, STEPS + 1):
        ref, base = (sums2, (n - 1) * 2 * CELLS) if n <= SECOND else (sums1, (n - 1 - SECOND) * 2 * CELLS)
        wave = waves[n - 1, :, :]
        for x, w in total:
            at = base + w * CELLS + x * DOM
            part = jnp.sum(ref[at : at + DOM, :], axis=0, keepdims=True)
            total[x, w] = total[x, w] + wave * jnp.sum(part, axis=1, keepdims=True)
    for x, w in total:
        for k in range(2):
            out_g[k, x, w : w + 1, :] = total[x, w][k : k + 1, :]


def call(kernel, name, out_shapes, inputs, smem=1, scratch=(), room=12, hbm=()):
    smem_spec, vmem_spec, hbm_spec = (pl.BlockSpec(memory_space=m) for m in (pltpu.SMEM, pltpu.VMEM, pltpu.HBM))
    return pl.pallas_call(
        kernel,
        out_shape=[jax.ShapeDtypeStruct(s, jnp.float32) for s in out_shapes],
        in_specs=[smem_spec if k < smem else hbm_spec if k in hbm else vmem_spec for k in range(len(inputs))],
        out_specs=[vmem_spec] * len(out_shapes),
        scratch_shapes=[pltpu.VMEM(s, jnp.float32) if isinstance(s, tuple) else s for s in scratch],
        compiler_params=pltpu.CompilerParams(vmem_limit_bytes=room << 20),
        name=name,
    )(*inputs)


def per_device(ckpt_e, ckpt_h, adj_e, adj_h, material, inv_perm, poling, freqs):
    assert material.shape == (CELLS, CELLS, LANES) and poling.shape == (2, 2)
    n_len, n_wid = (lax.axis_size("len"), lax.axis_size("wid"))
    my_len, my_wid = (lax.axis_index("len"), lax.axis_index("wid"))
    ids = jnp.stack([my_len % 2, my_len, my_wid]).astype(jnp.int32)

    def swap(value, axes, pairs):
        return lax.ppermute(value, axes, [p for i, j in pairs for p in ((i, j), (j, i))])

    def swap_a(value):
        return swap(value, "len", [(i, i + 1) for i in range(1, n_len - 1, 2)])

    def swap_b(value):
        return swap(value, "len", [(i, i + 1) for i in range(0, n_len, 2)])

    def swap_c(value):
        pairs = [(i * n_wid + w, (i + 1) * n_wid + w + 1) for i in range(0, n_len, 2) for w in range(n_wid - 1)]
        return swap(value, ("len", "wid"), pairs)

    raw = [x.reshape(3, CELLS * CELLS, LANES) for x in (ckpt_e, ckpt_h)]
    raw += [material.reshape(CELLS * CELLS, LANES)]
    raw += [x.reshape(3, CELLS * CELLS, LANES) for x in (adj_e, adj_h)]

    angle = math.pi / DOM * np.arange(DOM)
    n = np.arange(1, STEPS + 1)
    turn = np.stack([np.cos(OMEGA * n), np.sin(OMEGA * n)], 1)
    norm = 1.0 / math.sqrt(n_len * CELLS)
    partial = np.stack([np.cumsum(np.cos(angle)), np.cumsum(np.sin(angle))], 0)
    beta = jnp.asarray(np.broadcast_to((norm * turn @ partial)[:, :, None], (STEPS, DOM, LANES)), jnp.float32)
    alpha = tuple(float(v) for v in norm * turn @ partial[:, -1])
    phases = freqs[None, :] * jnp.arange(1, STEPS + 1, dtype=jnp.float32)[:, None]
    scale = 1.0 / math.sqrt(DOM * DOM * LANES)
    waves = scale * jnp.stack([jnp.cos(phases), -jnp.sin(phases)], axis=1)

    def spread(exchange, own, a, b, sent=None):
        one = functools.partial(kernel_c1, exchange)
        two = functools.partial(kernel_c2, exchange)
        a, b = (swap_a(a), swap_b(b))
        c1 = swap_c(call(one, "pack_rows", [(exchange.rows["c1"], LANES)], [ids, own, b])[0])
        env, extra = ([], 0)
        if sent is not None:
            sent, b = lax.optimization_barrier((sent, b))
            env, extra = ([jnp.sum(lax.all_to_all(sent, "len", 0, 0), axis=0)], 8)
            a, *env = lax.optimization_barrier((a, *env))
        a_other = swap_b(a)
        c2 = call(two, "pack_corners", [(exchange.rows["c2"] + extra, LANES)], [ids, own, a, a_other, *env])[0]
        c1, c2 = lax.optimization_barrier((c1, c2))
        c2 = swap_c(c2)
        return [a, a_other, b, c1, swap_b(c1), c2, swap_b(c2)], env

    own, a, b, sent = call(
        kernel_start,
        "start",
        [(13, CELLS * CELLS, LANES), (EX1.rows["a"], LANES), (EX1.rows["b"], LANES), (n_len, 8, LANES)],
        [ids, pltpu.with_memory_space_constraint(poling, pltpu.HBM), *[pltpu.with_memory_space_constraint(x, pltpu.HBM) for x in raw]],
        smem=2,
        hbm=range(2, 7),
        scratch=[(12, CELLS * CELLS, LANES), pltpu.VMEM((CELLS * CELLS, LANES), jnp.int32), pltpu.SemaphoreType.DMA((5,))],
    )
    messages, env = spread(EX1, own, a, b, sent)
    a, b, own2, coef_a, kept, sums, drive = call(
        functools.partial(kernel_first, alpha),
        "forward",
        [
            (EX2.rows["a"], LANES),
            (EX2.rows["b"], LANES),
            (6, CELLS * CELLS, LANES),
            (XAN * YAN, LANES),
            (SECOND, 3, YFN * XAN, LANES),
            (FIRST * 2 * CELLS, LANES),
            (STEPS, 4, XAN, LANES),
        ],
        [ids, inv_perm, own, *messages, *env, beta],
        smem=2,
        room=36,
        scratch=[
            (3, XN * YN, LANES),
            (3, XN * YN, LANES),
            (XN * YN, LANES),
            (XN * YN, LANES),
            (3, XAN * YAN, LANES),
            (3, XAN * YAN, LANES),
            (FIRST, 3, YFN * XAN, LANES),
            (YFN * XAN, LANES),
        ],
    )
    messages, _ = spread(EX2, own2, a, b)
    out_e, out_h, out_g = call(
        kernel_second,
        "adjoint",
        [(3, CELLS * CELLS, LANES), (3, CELLS * CELLS, LANES), (2, 2, 2, BINS)],
        [ids, own2, *messages, coef_a, kept, sums, drive, waves],
        room=18,
        scratch=[(3, XAN * YAN, LANES), (3, XAN * YAN, LANES), (SECOND * 2 * CELLS, LANES)],
    )
    shape = (3, CELLS, CELLS, LANES)
    return out_e.reshape(shape), out_h.reshape(shape), out_g.transpose(0, 3, 1, 2)


def solution(mesh):
    field = P(None, "len", "wid", None)
    in_specs = (field, field, field, field, P("len", "wid", None), P(), P("len", "wid"), P())
    out_specs = (field, field, P(None, None, "len", "wid"))
    return jax.shard_map(per_device, mesh=mesh, in_specs=in_specs, out_specs=out_specs, check_vma=False)
```

time: 367 us -> 98.9 us (0.27)
  the two profiles are of different devices: /device:TPU:7 before, /device:TPU:229 now
where the time goes in v1:
time: 98.9 us; the launch traced here: 98.6 us
  blocking collectives  36.5 us (37%)
  Pallas kernels  22.7 us (23%)
  waiting for transfers between devices  22.5 us (23%)
  starting transfers between devices  15.7 us (16%)
    all_to_all x1, blocking collectives, spread(): env, extra = ([jnp.sum(lax.all_to_all(sent, 'len', 0, 0), axis=0)], 8)  36.5 us
    pallas_call x7, Pallas kernels, call(): pl.pallas_call(kernel, out_shape=[jax.ShapeDtypeStruct(s, jnp.float32) fo...  22.7 us
    ppermute x14, waiting for transfers between devices, swap(): lax.ppermute(value, axes, [p for i, j in pairs for p in ((i, j), (j, i))])  22.5 us
    ppermute x14, starting transfers between devices, swap(): lax.ppermute(value, axes, [p for i, j in pairs for p in ((i, j), (j, i))])  15.7 us
  transfers between devices with their start and end apart: 14, of which 8 were waited for; matrix products, arithmetic and copies ran while one was open for 0% of the time, Pallas kernels for 4%

profile of v1, /device:TPU:229, one launch (start us, length us, event | category | flops | bytes accessed | tf_op | source)
XLA Modules:
  0.0 98.6 jit_solution(9591062691526773030)
XLA Ops:
  0.6 0.1 pad_add_fusion.ids
  0.7 3.3 %start.1 = (f32[13,256,128]{2,1,0:T(8,128)S(1)}, f32[1424,128]{1,0:T(8,128)}, f32[2000,128]{1,0:T(8,128)S(1)}, f32[16,8,128]{2,1,0:T(8,128)S(1)}) custom-call(s32[3]{0:T(128)S(1)} %pad_add_fusion.ids, s32[2,2]{1,0:T(2,128)} %poling.1, f32[3,256,128]{2,1,0:T(8,128)} %bitcast.12, f32[3,256,128]{2,1,0:T(8,128)} %bitcast.13, s32[256,128]{1,0:T(8,128)} %bitcast.16, ...), custom_call_target="tpu_custom_call" | custom-call | tf_op jit(solution)/shard_map/start/pallas_call | solution.py:522
  4.1 0.8 collective-permute-start.1
  4.8 2.7 %collective-permute-start = (f32[1424,128]{1,0:T(8,128)}, f32[1424,128]{1,0:T(8,128)S(1)}, u32[]{:S(2)}, u32[]{:S(2)}) collective-permute-start(f32[1424,128]{1,0:T(8,128)} %get-tuple-element.26), channel_id=1, source_target_pairs={{16,32},{32,16},{48,64},{64,48},{80,96},{96,80},{112,128},{128,112... | collective-permute-start | bytes 2187272 | tf_op jit(solution)/shard_map/ppermute | solution.py:540
  7.5 0.0 collective-permute-done.1.b.rest_2_
  7.6 1.8 %pack_rows.2 = f32[2848,128]{1,0:T(8,128)} custom-call(s32[3]{0:T(128)S(1)} %pad_add_fusion.ids, f32[13,256,128]{2,1,0:T(8,128)S(1)} %get-tuple-element.25.own, f32[2000,128]{1,0:T(8,128)S(1)} %collective-permute-done.1.b.rest_2_), custom_call_target="tpu_custom_call" | custom-call | tf_op jit(solution)/shard_map/pack_rows/pallas_call | solution.py:522
  9.3 2.4 %collective-permute-start.3 = (f32[2848,128]{1,0:T(8,128)}, f32[2848,128]{1,0:T(8,128)}, u32[]{:S(2)}, u32[]{:S(2)}) collective-permute-start(f32[2848,128]{1,0:T(8,128)} %pack_rows.2), channel_id=1, source_target_pairs={{0,17},{17,0},{1,18},{18,1},{2,19},{19,2},{3,20},{20,3},{4,21},{21... | collective-permute-start | bytes 4374536 | tf_op jit(solution)/shard_map/ppermute | solution.py:540
  11.7 36.5 %all_to_all.5 = f32[16,8,128]{2,1,0:T(8,128)S(1)} all-to-all(f32[16,8,128]{2,1,0:T(8,128)S(1)} %get-tuple-element.29), channel_id=1, replica_groups=mesh['len'=16,'wid'=16] {'len'}, dimensions={0} | all-to-all | bytes 131072 | tf_op jit(solution)/shard_map/all_to_all | solution.py:575
  48.2 0.0 copy-start
  48.2 0.0 copy-start.1
  48.2 0.0 collective-permute-done.a.rest_0_
  48.2 0.9 collective-permute-start.2
  49.1 1.8 %collective-permute-done.2.a_other.rest_1_ = f32[1424,128]{1,0:T(8,128)S(1)} collective-permute-done((f32[1424,128]{1,0:T(8,128)S(1)}, f32[1424,128]{1,0:T(8,128)S(1)}, u32[]{:S(2)}, u32[]{:S(2)}) %collective-permute-start.2) | collective-permute-done | bytes 729120 | tf_op jit(solution)/shard_map/ppermute | solution.py:540
  51.0 0.6 pack_corners.2
  51.6 0.0 collective-permute-done.3.rest_3_
  51.6 0.5 collective-permute-start.4
  52.0 1.9 %collective-permute-start.5 = (f32[736,128]{1,0:T(8,128)S(1)}, f32[736,128]{1,0:T(8,128)S(1)}, u32[]{:S(2)}, u32[]{:S(2)}) collective-permute-start(f32[736,128]{1,0:T(8,128)S(1)} %pack_corners.2), channel_id=1, source_target_pairs={{0,17},{17,0},{1,18},{18,1},{2,19},{19,2},{3,20},{20,3},{4,21},{21... | collective-permute-start | bytes 1130504 | tf_op jit(solution)/shard_map/ppermute | solution.py:540
  54.0 7.0 %collective-permute-done.5.rest_5_ = f32[736,128]{1,0:T(8,128)S(1)} collective-permute-done((f32[736,128]{1,0:T(8,128)S(1)}, f32[736,128]{1,0:T(8,128)S(1)}, u32[]{:S(2)}, u32[]{:S(2)}) %collective-permute-start.5) | collective-permute-done | bytes 376864 | tf_op jit(solution)/shard_map/ppermute | solution.py:540
  61.0 0.0 collective-permute-start.6
  61.0 1.7 %collective-permute-done.6.rest_6_ = f32[736,128]{1,0:T(8,128)S(1)} collective-permute-done((f32[736,128]{1,0:T(8,128)S(1)}, f32[736,128]{1,0:T(8,128)S(1)}, u32[]{:S(2)}, u32[]{:S(2)}) %collective-permute-start.6) | collective-permute-done | bytes 376864 | tf_op jit(solution)/shard_map/ppermute | solution.py:540
  62.7 0.0 collective-permute-done.4.rest_4_
  62.7 0.0 copy-done
  62.7 0.0 copy-done.1
  62.7 10.7 %forward.1 = (f32[464,128]{1,0:T(8,128)S(1)}, f32[760,128]{1,0:T(8,128)S(1)}, f32[6,256,128]{2,1,0:T(8,128)S(1)}, f32[1280,128]{1,0:T(8,128)S(1)}, f32[5,3,832,1...) custom-call(s32[3]{0:T(128)S(1)} %pad_add_fusion.ids, f32[4]{0:T(128)S(1)} %copy-done.1, ...), custom_call_target="tpu_custom_call" | custom-call | tf_op jit(solution)/shard_map/forward/pallas_call | solution.py:522
  73.4 0.2 collective-permute-start.9
  73.6 2.3 %collective-permute-start.7 = (f32[464,128]{1,0:T(8,128)S(1)}, f32[464,128]{1,0:T(8,128)S(1)}, u32[]{:S(2)}, u32[]{:S(2)}) collective-permute-start(f32[464,128]{1,0:T(8,128)S(1)} %get-tuple-element.36), channel_id=1, source_target_pairs={{16,32},{32,16},{48,64},{64,48},{80,96},{96,80},{112,128},{128,112... | collective-permute-start | bytes 712712 | tf_op jit(solution)/shard_map/ppermute | solution.py:540
  76.0 0.0 collective-permute-done.9.b.rest_2_
  76.0 0.0 copy-start.2
  76.0 0.6 pack_rows.3
  76.6 1.9 %collective-permute-start.10 = (f32[928,128]{1,0:T(8,128)S(1)}, f32[928,128]{1,0:T(8,128)S(1)}, u32[]{:S(2)}, u32[]{:S(2)}) collective-permute-start(f32[928,128]{1,0:T(8,128)S(1)} %pack_rows.3), channel_id=1, source_target_pairs={{0,17},{17,0},{1,18},{18,1},{2,19},{19,2},{3,20},{20,3},{4,21},{21... | collective-permute-start | bytes 1425416 | tf_op jit(solution)/shard_map/ppermute | solution.py:540
  78.5 4.9 %collective-permute-done.7.a.rest_0_ = f32[464,128]{1,0:T(8,128)S(1)} collective-permute-done((f32[464,128]{1,0:T(8,128)S(1)}, f32[464,128]{1,0:T(8,128)S(1)}, u32[]{:S(2)}, u32[]{:S(2)}) %collective-permute-start.7) | collective-permute-done | bytes 237600 | tf_op jit(solution)/shard_map/ppermute | solution.py:540
  83.5 0.0 collective-permute-start.8
  83.5 1.5 %collective-permute-done.8.a_other.rest_1_ = f32[464,128]{1,0:T(8,128)S(1)} collective-permute-done((f32[464,128]{1,0:T(8,128)S(1)}, f32[464,128]{1,0:T(8,128)S(1)}, u32[]{:S(2)}, u32[]{:S(2)}) %collective-permute-start.8) | collective-permute-done | bytes 237600 | tf_op jit(solution)/shard_map/ppermute | solution.py:540
  85.0 0.6 pack_corners.3
  85.5 1.0 %collective-permute-done.10.rest_3_ = f32[928,128]{1,0:T(8,128)S(1)} collective-permute-done((f32[928,128]{1,0:T(8,128)S(1)}, f32[928,128]{1,0:T(8,128)S(1)}, u32[]{:S(2)}, u32[]{:S(2)}) %collective-permute-start.10) | collective-permute-done | bytes 475168 | tf_op jit(solution)/shard_map/ppermute | solution.py:540
  86.6 0.0 collective-permute-start.11
  86.6 2.0 %collective-permute-start.12 = (f32[128,128]{1,0:T(8,128)S(1)}, f32[128,128]{1,0:T(8,128)S(1)}, u32[]{:S(2)}, u32[]{:S(2)}) collective-permute-start(f32[128,128]{1,0:T(8,128)S(1)} %pack_corners.3), channel_id=1, source_target_pairs={{0,17},{17,0},{1,18},{18,1},{2,19},{19,2},{3,20},{20,3},{4,21},{21... | collective-permute-start | bytes 196616 | tf_op jit(solution)/shard_map/ppermute | solution.py:540
  88.6 0.0 copy-done.2
  88.6 0.2 multiply_cosine_fusion
  88.8 3.3 %collective-permute-done.12.rest_5_ = f32[128,128]{1,0:T(8,128)S(1)} collective-permute-done((f32[128,128]{1,0:T(8,128)S(1)}, f32[128,128]{1,0:T(8,128)S(1)}, u32[]{:S(2)}, u32[]{:S(2)}) %collective-permute-start.12) | collective-permute-done | bytes 65568 | tf_op jit(solution)/shard_map/ppermute | solution.py:540
  92.2 0.0 collective-permute-start.13
  92.2 1.2 %collective-permute-done.13.rest_6_ = f32[128,128]{1,0:T(8,128)S(1)} collective-permute-done((f32[128,128]{1,0:T(8,128)S(1)}, f32[128,128]{1,0:T(8,128)S(1)}, u32[]{:S(2)}, u32[]{:S(2)}) %collective-permute-start.13) | collective-permute-done | bytes 65568 | tf_op jit(solution)/shard_map/ppermute | solution.py:540
  93.4 0.0 collective-permute-done.11.rest_4_
  93.4 5.1 %adjoint.1 = (f32[3,256,128]{2,1,0:T(8,128)}, f32[3,256,128]{2,1,0:T(8,128)}, f32[2,2,2,8]{3,2,1,0:T(2,128)}) custom-call(s32[3]{0:T(128)S(1)} %pad_add_fusion.ids, f32[6,256,128]{2,1,0:T(8,128)S(1)} %get-tuple-element.35.own, f32[464,128]{1,0:T(8,128)S(1)} %collective-permute-done.7.a.rest_0_, f32[464,128]{1,0:T(8,128)S(1)} %collective-permute-done.8.a_other.rest_1_, ...), custom_call_target="tpu_custom_call" | custom-call | tf_op jit(solution)/shard_map/adjoint/pallas_call | solution.py:522
  (4 shorter events, 0.0 us)
Async XLA Ops:
  4.1 3.5 %collective-permute-start.1 = (f32[2000,128]{1,0:T(8,128)S(1)}, f32[2000,128]{1,0:T(8,128)S(1)}, u32[]{:S(2)}, u32[]{:S(2)}) collective-permute-start(f32[2000,128]{1,0:T(8,128)S(1)} %get-tuple-element.28), channel_id=1, source_target_pairs={{0,16},{16,0},{32,48},{48,32},{64,80},{80,64},{96,112},{112,96},{1... | collective-permute-start | bytes 3072008 | tf_op jit(solution)/shard_map/ppermute | solution.py:540
  4.8 43.4 %collective-permute-start = (f32[1424,128]{1,0:T(8,128)}, f32[1424,128]{1,0:T(8,128)S(1)}, u32[]{:S(2)}, u32[]{:S(2)}) collective-permute-start(f32[1424,128]{1,0:T(8,128)} %get-tuple-element.26), channel_id=1, source_target_pairs={{16,32},{32,16},{48,64},{64,48},{80,96},{96,80},{112,128},{128,112... | collective-permute-start | bytes 2187272 | tf_op jit(solution)/shard_map/ppermute | solution.py:540
  9.3 42.3 %collective-permute-start.3 = (f32[2848,128]{1,0:T(8,128)}, f32[2848,128]{1,0:T(8,128)}, u32[]{:S(2)}, u32[]{:S(2)}) collective-permute-start(f32[2848,128]{1,0:T(8,128)} %pack_rows.2), channel_id=1, source_target_pairs={{0,17},{17,0},{1,18},{18,1},{2,19},{19,2},{3,20},{20,3},{4,21},{21... | collective-permute-start | bytes 4374536 | tf_op jit(solution)/shard_map/ppermute | solution.py:540
  48.2 14.5 %copy-start = (f32[8,8,128]{2,1,0:T(8,128)S(1)}, f32[8,8,128]{2,1,0:T(8,128)}, u32[]{:S(2)}) copy-start(f32[8,8,128]{2,1,0:T(8,128)} %constant.28.clone.rest_8_) | copy-start | bytes 98308
  48.2 14.4 %copy-start.1 = (f32[4]{0:T(128)S(1)}, f32[4]{0:T(128)}, u32[]{:S(2)}) copy-start(f32[4]{0:T(128)} %perm.1) | copy-start | bytes 52
  48.2 2.7 %collective-permute-start.2 = (f32[1424,128]{1,0:T(8,128)S(1)}, f32[1424,128]{1,0:T(8,128)S(1)}, u32[]{:S(2)}, u32[]{:S(2)}) collective-permute-start(f32[1424,128]{1,0:T(8,128)S(1)} %collective-permute-done.a.rest_0_), channel_id=1, source_target_pairs={{0,16},{16,0},{32,48},{48,32},{64,80},{80,64},{96,112},{112,96},{1... | collective-permute-start | bytes 2187272 | tf_op jit(solution)/shard_map/ppermute | solution.py:540
  51.6 11.1 %collective-permute-start.4 = (f32[2848,128]{1,0:T(8,128)}, f32[2848,128]{1,0:T(8,128)S(1)}, u32[]{:S(2)}, u32[]{:S(2)}) collective-permute-start(f32[2848,128]{1,0:T(8,128)} %collective-permute-done.3.rest_3_), channel_id=1, source_target_pairs={{0,16},{16,0},{32,48},{48,32},{64,80},{80,64},{96,112},{112,96},{1... | collective-permute-start | bytes 4374536 | tf_op jit(solution)/shard_map/ppermute | solution.py:540
  52.0 8.9 %collective-permute-start.5 = (f32[736,128]{1,0:T(8,128)S(1)}, f32[736,128]{1,0:T(8,128)S(1)}, u32[]{:S(2)}, u32[]{:S(2)}) collective-permute-start(f32[736,128]{1,0:T(8,128)S(1)} %pack_corners.2), channel_id=1, source_target_pairs={{0,17},{17,0},{1,18},{18,1},{2,19},{19,2},{3,20},{20,3},{4,21},{21... | collective-permute-start | bytes 1130504 | tf_op jit(solution)/shard_map/ppermute | solution.py:540
  61.0 1.7 %collective-permute-start.6 = (f32[736,128]{1,0:T(8,128)S(1)}, f32[736,128]{1,0:T(8,128)S(1)}, u32[]{:S(2)}, u32[]{:S(2)}) collective-permute-start(f32[736,128]{1,0:T(8,128)S(1)} %collective-permute-done.5.rest_5_), channel_id=1, source_target_pairs={{0,16},{16,0},{32,48},{48,32},{64,80},{80,64},{96,112},{112,96},{1... | collective-permute-start | bytes 1130504 | tf_op jit(solution)/shard_map/ppermute | solution.py:540
  73.4 2.6 %collective-permute-start.9 = (f32[760,128]{1,0:T(8,128)S(1)}, f32[760,128]{1,0:T(8,128)S(1)}, u32[]{:S(2)}, u32[]{:S(2)}) collective-permute-start(f32[760,128]{1,0:T(8,128)S(1)} %get-tuple-element.37), channel_id=1, source_target_pairs={{0,16},{16,0},{32,48},{48,32},{64,80},{80,64},{96,112},{112,96},{1... | collective-permute-start | bytes 1167368 | tf_op jit(solution)/shard_map/ppermute | solution.py:540
  73.6 9.8 %collective-permute-start.7 = (f32[464,128]{1,0:T(8,128)S(1)}, f32[464,128]{1,0:T(8,128)S(1)}, u32[]{:S(2)}, u32[]{:S(2)}) collective-permute-start(f32[464,128]{1,0:T(8,128)S(1)} %get-tuple-element.36), channel_id=1, source_target_pairs={{16,32},{32,16},{48,64},{64,48},{80,96},{96,80},{112,128},{128,112... | collective-permute-start | bytes 712712 | tf_op jit(solution)/shard_map/ppermute | solution.py:540
  76.0 12.6 %copy-start.2 = (f32[8]{0:T(128)S(1)}, f32[8]{0:T(128)}, u32[]{:S(2)}) copy-start(f32[8]{0:T(128)} %param.16) | copy-start | bytes 100
  76.6 10.0 %collective-permute-start.10 = (f32[928,128]{1,0:T(8,128)S(1)}, f32[928,128]{1,0:T(8,128)S(1)}, u32[]{:S(2)}, u32[]{:S(2)}) collective-permute-start(f32[928,128]{1,0:T(8,128)S(1)} %pack_rows.3), channel_id=1, source_target_pairs={{0,17},{17,0},{1,18},{18,1},{2,19},{19,2},{3,20},{20,3},{4,21},{21... | collective-permute-start | bytes 1425416 | tf_op jit(solution)/shard_map/ppermute | solution.py:540
  83.5 1.5 %collective-permute-start.8 = (f32[464,128]{1,0:T(8,128)S(1)}, f32[464,128]{1,0:T(8,128)S(1)}, u32[]{:S(2)}, u32[]{:S(2)}) collective-permute-start(f32[464,128]{1,0:T(8,128)S(1)} %collective-permute-done.7.a.rest_0_), channel_id=1, source_target_pairs={{0,16},{16,0},{32,48},{48,32},{64,80},{80,64},{96,112},{112,96},{1... | collective-permute-start | bytes 712712 | tf_op jit(solution)/shard_map/ppermute | solution.py:540
  86.6 6.9 %collective-permute-start.11 = (f32[928,128]{1,0:T(8,128)S(1)}, f32[928,128]{1,0:T(8,128)S(1)}, u32[]{:S(2)}, u32[]{:S(2)}) collective-permute-start(f32[928,128]{1,0:T(8,128)S(1)} %collective-permute-done.10.rest_3_), channel_id=1, source_target_pairs={{0,16},{16,0},{32,48},{48,32},{64,80},{80,64},{96,112},{112,96},{1... | collective-permute-start | bytes 1425416 | tf_op jit(solution)/shard_map/ppermute | solution.py:540
  86.6 5.6 %collective-permute-start.12 = (f32[128,128]{1,0:T(8,128)S(1)}, f32[128,128]{1,0:T(8,128)S(1)}, u32[]{:S(2)}, u32[]{:S(2)}) collective-permute-start(f32[128,128]{1,0:T(8,128)S(1)} %pack_corners.3), channel_id=1, source_target_pairs={{0,17},{17,0},{1,18},{18,1},{2,19},{19,2},{3,20},{20,3},{4,21},{21... | collective-permute-start | bytes 196616 | tf_op jit(solution)/shard_map/ppermute | solution.py:540
  92.2 1.3 %collective-permute-start.13 = (f32[128,128]{1,0:T(8,128)S(1)}, f32[128,128]{1,0:T(8,128)S(1)}, u32[]{:S(2)}, u32[]{:S(2)}) collective-permute-start(f32[128,128]{1,0:T(8,128)S(1)} %collective-permute-done.12.rest_5_), channel_id=1, source_target_pairs={{0,16},{16,0},{32,48},{48,32},{64,80},{80,64},{96,112},{112,96},{1... | collective-permute-start | bytes 196616 | tf_op jit(solution)/shard_map/ppermute | solution.py:540

commit v2 on v1

--- a/solution.py
+++ b/solution.py
@@ -223,7 +223,7 @@
 
 def columns_loop(first, last, vregs, body):
     count = last - first
-    trips = max(1, round(count * vregs / 110))
+    trips = max(1, round(count * vregs / 180))
     group = -(-count // trips)
     trips = -(-count // group)
     if trips == 1:
@@ -312,36 +312,46 @@
                 magnetic[c, (-1 - yo) * xn : -yo * xn, :] = zero
 
 
-def adjoint_steps(ids, numbers, needs, electric, magnetic, coef, kept, drive, sums, sum_row):
+def adjoint_steps(ids, numbers, needs, electric, magnetic, coef, kept, drive, products, sums, sum_row):
     window = (XA, XAN, YA, YAN)
     for done, n in enumerate(numbers):
         left = len(numbers) - done
-        bounds = needs[4][left]
-        _, _, y0, y1 = bounds
+        x0, x1, y0, y1 = needs[4][left]
+        offset, count = rows_of((x0, x1), XA, XAN)
         field = kept(n)
+        first = lax.broadcasted_iota(jnp.int32, (count, LANES), 1) == 0
         for y in range(y0, y1):
-            factor = drive[n - 1, y // DOM + 1, :, :]
-            at, at_kept = ((y - YA) * XAN, (y - YF) * XAN)
-            total = None
+            row = (y - YA) * XAN + offset
+            here, down_x, down_y = (slice(row - d, row - d + count) for d in (0, 1, XAN))
+            at = (y - YF) * XAN + offset
+            factor = drive[n - 1, y // DOM + 1, offset : offset + count, :]
+            values = [field[c, at : at + count, :] for c in range(3)]
+            new = [electric[c, here, :] + factor * values[c] for c in range(3)]
+            if 0 <= y < CELLS:
+                products[y * XAN + offset : y * XAN + offset + count, :] = (
+                    new[0] * values[0] + new[1] * values[1] + new[2] * values[2]
+                )
+            hx, hy, hz = (magnetic[c, here, :] for c in range(3))
+            hy_z = hy - jnp.where(first, 0.0, pltpu.roll(hy, 1, 1))
+            hx_z = hx - jnp.where(first, 0.0, pltpu.roll(hx, 1, 1))
+            curl = (
+                (hz - magnetic[2, down_y, :]) - hy_z,
+                hx_z - (hz - magnetic[2, down_x, :]),
+                (hy - magnetic[1, down_x, :]) - (hx - magnetic[0, down_y, :]),
+            )
+            scale = coef[here, :]
             for c in range(3):
-                value = field[c, at_kept : at_kept + XAN, :]
-                new = electric[c, at : at + XAN, :] + factor * value
-                electric[c, at : at + XAN, :] = new
-                term = new * value
-                total = term if total is None else total + term
-            if 0 <= y < CELLS:
-                slot = sum_row(n) + (y // DOM) * CELLS
-                part = total[-XA : CELLS - XA, :]
-                if y % DOM == 0:
-                    acc = part
-                else:
-                    acc = acc + part
-                if y % DOM == DOM - 1:
-                    sums[slot : slot + CELLS, :] = acc
-        electric_pass(magnetic, electric, coef, -1, bounds, window)
+                electric[c, here, :] = new[c] - scale * curl[c]
         after = needs[5][left]
         magnetic_pass(electric, magnetic, 1, after, window)
         clear_outside(ids, magnetic, after, window)
+        for w in range(2):
+            total = None
+            for y in range(w * DOM, (w + 1) * DOM):
+                part = products[y * XAN - XA : y * XAN - XA + CELLS, :]
+                total = part if total is None else total + part
+            slot = sum_row(n) + w * CELLS
+            sums[slot : slot + CELLS, :] = total
 
 
 def both_cores(ids, work):
@@ -366,13 +376,13 @@
     mine = jnp.where(lane < 64, before, here)
     for k in range(sent.shape[0]):
         sent[k, :, :] = mine
-    for k, (first, count) in enumerate(((0, 3), (3, 3), (6, 1), (7, 3), (10, 3))):
-        copies[k].wait()
-        for f in range(first, first + count):
-            for y in range(CELLS):
-                rows = pl.ds(y, CELLS, stride=CELLS)
-                value = raw_m[rows, :].astype(jnp.float32) + 1.0 if f == 6 else raw[f if f < 6 else f - 1, rows, :]
-                own[f, y * CELLS : (y + 1) * CELLS, :] = value
+    for f in range(13):
+        if f in (0, 3, 6, 7, 10):
+            copies[(0, 3, 6, 7, 10).index(f)].wait()
+        for y in range(CELLS):
+            rows = pl.ds(y, CELLS, stride=CELLS)
+            value = raw_m[rows, :].astype(jnp.float32) + 1.0 if f == 6 else raw[f if f < 6 else f - 1, rows, :]
+            own[f, y * CELLS : (y + 1) * CELLS, :] = value
 
     def work(core):
         pack_a(core, EX1, own, out_a)
@@ -412,7 +422,7 @@
 
 def kernel_first(alpha, ids, perm, own, *rest):
     refs = dict(zip(NAMES, rest))
-    (env, beta, out_a, out_b, own2, coef_a, kept, sums, drive, ef, hf, mf, coef, ea, ga, late, chi) = rest[len(NAMES) :]
+    (env, beta, out_a, out_b, own2, coef_a, kept, sums, drive, ef, hf, mf, coef, ea, ga, late, chi, products) = rest[len(NAMES) :]
 
     def store(f, y, x, value):
         count = value.shape[0]
@@ -459,21 +469,17 @@
         magnetic_pass(ef, hf, -1, FWD[4][n], window)
         clear_outside(ids, hf, FWD[4][n], window)
         electric_pass(hf, ef, coef, 1, FWD[3][n], window)
-        _, _, y0, y1 = FWD[5][n]
+        x0, x1, y0, y1 = FWD[5][n]
+        skip, count = rows_of((x0, x1), XA, XAN)
         target = kept.at[n - 1] if n <= SECOND else late.at[n - 1 - SECOND]
 
-        def keep(start, group, y0=y0, target=target):
-            for j in range(group):
-                rows = pl.ds((start + (j + y0 - YO)) * XN + XA - XO, XAN)
-                to = pl.ds((start + (j + y0 - YF)) * XAN, XAN)
-                mask = chi[to, :]
-                for k in range(3):
-                    target[k, to, :] = ef[k, rows, :] * mask
-
-        for y in range(0, y1 - y0):
-            keep(y, 1)
-
-    adjoint_steps(ids, list(range(STEPS, SECOND, -1)), ADJ1, ea, ga, coef_a, lambda n: late.at[n - 1 - SECOND], drive, sums,
+        for y in range(y0, y1):
+            at, to = ((y - YO) * XN + XA - XO + skip, (y - YF) * XAN + skip)
+            mask = chi[to : to + count, :]
+            for k in range(3):
+                target[k, to : to + count, :] = ef[k, at : at + count, :] * mask
+
+    adjoint_steps(ids, list(range(STEPS, SECOND, -1)), ADJ1, ea, ga, coef_a, lambda n: late.at[n - 1 - SECOND], drive, products, sums,
                   lambda n: (n - 1 - SECOND) * 2 * CELLS)
     for y in range(CELLS):
         at = (y - YA) * XAN - XA
@@ -490,14 +496,14 @@
 
 def kernel_second(ids, own, *rest):
     refs = dict(zip(NAMES, rest))
-    coef_a, kept, sums1, drive, waves, out_e, out_h, out_g, ea, ga, sums2 = rest[len(NAMES) :]
+    coef_a, kept, sums1, drive, waves, out_e, out_h, out_g, ea, ga, sums2, products = rest[len(NAMES) :]
 
     def store(f, y, x, value):
         row = (y - YA) * XAN + x - XA
         (ea if f < 3 else ga)[f % 3, row : row + value.shape[0], :] = value
 
     both_cores(ids, lambda core: unpack(core, EX2, NEEDS2, own, refs, store))
-    adjoint_steps(ids, list(range(SECOND, 0, -1)), ADJ2, ea, ga, coef_a, lambda n: kept.at[n - 1], drive, sums2,
+    adjoint_steps(ids, list(range(SECOND, 0, -1)), ADJ2, ea, ga, coef_a, lambda n: kept.at[n - 1], drive, products, sums2,
                   lambda n: (n - 1) * 2 * CELLS)
     for x in range(CELLS):
         for k in range(3):
@@ -614,6 +620,7 @@
             (3, XAN * YAN, LANES),
             (FIRST, 3, YFN * XAN, LANES),
             (YFN * XAN, LANES),
+            (CELLS * XAN, LANES),
         ],
     )
     messages, _ = spread(EX2, own2, a, b)
@@ -623,7 +630,7 @@
         [(3, CELLS * CELLS, LANES), (3, CELLS * CELLS, LANES), (2, 2, 2, BINS)],
         [ids, own2, *messages, coef_a, kept, sums, drive, waves],
         room=18,
-        scratch=[(3, XAN * YAN, LANES), (3, XAN * YAN, LANES), (SECOND * 2 * CELLS, LANES)],
+        scratch=[(3, XAN * YAN, LANES), (3, XAN * YAN, LANES), (SECOND * 2 * CELLS, LANES), (CELLS * XAN, LANES)],
     )
     shape = (3, CELLS, CELLS, LANES)
     return out_e.reshape(shape), out_h.reshape(shape), out_g.transpose(0, 3, 1, 2)

time: 98.9 us -> 97.8 us (0.989)
  Pallas kernels: 22.7 us -> 21.6 us
    pallas_call x7, Pallas kernels: 22.7 us -> 21.6 us  [call(): pl.pallas_call(kernel, out_shape=[jax.ShapeDtypeStruct(s, jnp.float32) fo...]
where the time goes in v2:
time: 97.8 us; the launch traced here: 97.5 us
  blocking collectives  36.5 us (37%)
  waiting for transfers between devices  22.5 us (23%)
  Pallas kernels  21.6 us (22%)
  starting transfers between devices  15.7 us (16%)
    all_to_all x1, blocking collectives, spread(): env, extra = ([jnp.sum(lax.all_to_all(sent, 'len', 0, 0), axis=0)], 8)  36.5 us
    ppermute x14, waiting for transfers between devices, swap(): lax.ppermute(value, axes, [p for i, j in pairs for p in ((i, j), (j, i))])  22.5 us
    pallas_call x7, Pallas kernels, call(): pl.pallas_call(kernel, out_shape=[jax.ShapeDtypeStruct(s, jnp.float32) fo...  21.6 us
    ppermute x14, starting transfers between devices, swap(): lax.ppermute(value, axes, [p for i, j in pairs for p in ((i, j), (j, i))])  15.7 us
  transfers between devices with their start and end apart: 14, of which 8 were waited for; matrix products, arithmetic and copies ran while one was open for 0% of the time, Pallas kernels for 4%

profile of v2, /device:TPU:229, one launch (start us, length us, event | category | flops | bytes accessed | tf_op | source)
XLA Modules:
  0.0 97.5 jit_solution(10701914363565939796)
XLA Ops:
  0.6 0.1 pad_add_fusion.ids
  0.7 3.3 %start.1 = (f32[13,256,128]{2,1,0:T(8,128)S(1)}, f32[1424,128]{1,0:T(8,128)}, f32[2000,128]{1,0:T(8,128)S(1)}, f32[16,8,128]{2,1,0:T(8,128)S(1)}) custom-call(s32[3]{0:T(128)S(1)} %pad_add_fusion.ids, s32[2,2]{1,0:T(2,128)} %poling.1, f32[3,256,128]{2,1,0:T(8,128)} %bitcast.12, f32[3,256,128]{2,1,0:T(8,128)} %bitcast.13, s32[256,128]{1,0:T(8,128)} %bitcast.16, ...), custom_call_target="tpu_custom_call" | custom-call | tf_op jit(solution)/shard_map/start/pallas_call | solution.py:528
  4.1 0.8 collective-permute-start.1
  4.8 2.7 %collective-permute-start = (f32[1424,128]{1,0:T(8,128)}, f32[1424,128]{1,0:T(8,128)S(1)}, u32[]{:S(2)}, u32[]{:S(2)}) collective-permute-start(f32[1424,128]{1,0:T(8,128)} %get-tuple-element.26), channel_id=1, source_target_pairs={{16,32},{32,16},{48,64},{64,48},{80,96},{96,80},{112,128},{128,112... | collective-permute-start | bytes 2187272 | tf_op jit(solution)/shard_map/ppermute | solution.py:546
  7.5 0.0 collective-permute-done.1.b.rest_2_
  7.6 1.8 %pack_rows.2 = f32[2848,128]{1,0:T(8,128)} custom-call(s32[3]{0:T(128)S(1)} %pad_add_fusion.ids, f32[13,256,128]{2,1,0:T(8,128)S(1)} %get-tuple-element.25.own, f32[2000,128]{1,0:T(8,128)S(1)} %collective-permute-done.1.b.rest_2_), custom_call_target="tpu_custom_call" | custom-call | tf_op jit(solution)/shard_map/pack_rows/pallas_call | solution.py:528
  9.3 2.4 %collective-permute-start.3 = (f32[2848,128]{1,0:T(8,128)}, f32[2848,128]{1,0:T(8,128)}, u32[]{:S(2)}, u32[]{:S(2)}) collective-permute-start(f32[2848,128]{1,0:T(8,128)} %pack_rows.2), channel_id=1, source_target_pairs={{0,17},{17,0},{1,18},{18,1},{2,19},{19,2},{3,20},{20,3},{4,21},{21... | collective-permute-start | bytes 4374536 | tf_op jit(solution)/shard_map/ppermute | solution.py:546
  11.7 36.5 %all_to_all.5 = f32[16,8,128]{2,1,0:T(8,128)S(1)} all-to-all(f32[16,8,128]{2,1,0:T(8,128)S(1)} %get-tuple-element.29), channel_id=1, replica_groups=mesh['len'=16,'wid'=16] {'len'}, dimensions={0} | all-to-all | bytes 131072 | tf_op jit(solution)/shard_map/all_to_all | solution.py:581
  48.2 0.0 copy-start
  48.2 0.0 copy-start.1
  48.2 0.0 collective-permute-done.a.rest_0_
  48.2 0.9 collective-permute-start.2
  49.1 1.8 %collective-permute-done.2.a_other.rest_1_ = f32[1424,128]{1,0:T(8,128)S(1)} collective-permute-done((f32[1424,128]{1,0:T(8,128)S(1)}, f32[1424,128]{1,0:T(8,128)S(1)}, u32[]{:S(2)}, u32[]{:S(2)}) %collective-permute-start.2) | collective-permute-done | bytes 729120 | tf_op jit(solution)/shard_map/ppermute | solution.py:546
  51.0 0.6 pack_corners.2
  51.6 0.0 collective-permute-done.3.rest_3_
  51.6 0.5 collective-permute-start.4
  52.0 1.9 %collective-permute-start.5 = (f32[736,128]{1,0:T(8,128)S(1)}, f32[736,128]{1,0:T(8,128)S(1)}, u32[]{:S(2)}, u32[]{:S(2)}) collective-permute-start(f32[736,128]{1,0:T(8,128)S(1)} %pack_corners.2), channel_id=1, source_target_pairs={{0,17},{17,0},{1,18},{18,1},{2,19},{19,2},{3,20},{20,3},{4,21},{21... | collective-permute-start | bytes 1130504 | tf_op jit(solution)/shard_map/ppermute | solution.py:546
  54.0 7.0 %collective-permute-done.5.rest_5_ = f32[736,128]{1,0:T(8,128)S(1)} collective-permute-done((f32[736,128]{1,0:T(8,128)S(1)}, f32[736,128]{1,0:T(8,128)S(1)}, u32[]{:S(2)}, u32[]{:S(2)}) %collective-permute-start.5) | collective-permute-done | bytes 376864 | tf_op jit(solution)/shard_map/ppermute | solution.py:546
  61.0 0.0 collective-permute-start.6
  61.0 1.7 %collective-permute-done.6.rest_6_ = f32[736,128]{1,0:T(8,128)S(1)} collective-permute-done((f32[736,128]{1,0:T(8,128)S(1)}, f32[736,128]{1,0:T(8,128)S(1)}, u32[]{:S(2)}, u32[]{:S(2)}) %collective-permute-start.6) | collective-permute-done | bytes 376864 | tf_op jit(solution)/shard_map/ppermute | solution.py:546
  62.7 0.0 collective-permute-done.4.rest_4_
  62.7 0.0 copy-done
  62.7 0.0 copy-done.1
  62.7 9.9 %forward.1 = (f32[464,128]{1,0:T(8,128)S(1)}, f32[760,128]{1,0:T(8,128)S(1)}, f32[6,256,128]{2,1,0:T(8,128)S(1)}, f32[1280,128]{1,0:T(8,128)S(1)}, f32[5,3,832,1...) custom-call(s32[3]{0:T(128)S(1)} %pad_add_fusion.ids, f32[4]{0:T(128)S(1)} %copy-done.1, ...), custom_call_target="tpu_custom_call" | custom-call | tf_op jit(solution)/shard_map/forward/pallas_call | solution.py:528
  72.6 0.2 collective-permute-start.9
  72.8 2.4 %collective-permute-start.7 = (f32[464,128]{1,0:T(8,128)S(1)}, f32[464,128]{1,0:T(8,128)S(1)}, u32[]{:S(2)}, u32[]{:S(2)}) collective-permute-start(f32[464,128]{1,0:T(8,128)S(1)} %get-tuple-element.36), channel_id=1, source_target_pairs={{16,32},{32,16},{48,64},{64,48},{80,96},{96,80},{112,128},{128,112... | collective-permute-start | bytes 712712 | tf_op jit(solution)/shard_map/ppermute | solution.py:546
  75.2 0.0 collective-permute-done.9.b.rest_2_
  75.2 0.0 copy-start.2
  75.2 0.6 pack_rows.3
  75.8 1.9 %collective-permute-start.10 = (f32[928,128]{1,0:T(8,128)S(1)}, f32[928,128]{1,0:T(8,128)S(1)}, u32[]{:S(2)}, u32[]{:S(2)}) collective-permute-start(f32[928,128]{1,0:T(8,128)S(1)} %pack_rows.3), channel_id=1, source_target_pairs={{0,17},{17,0},{1,18},{18,1},{2,19},{19,2},{3,20},{20,3},{4,21},{21... | collective-permute-start | bytes 1425416 | tf_op jit(solution)/shard_map/ppermute | solution.py:546
  77.7 4.9 %collective-permute-done.7.a.rest_0_ = f32[464,128]{1,0:T(8,128)S(1)} collective-permute-done((f32[464,128]{1,0:T(8,128)S(1)}, f32[464,128]{1,0:T(8,128)S(1)}, u32[]{:S(2)}, u32[]{:S(2)}) %collective-permute-start.7) | collective-permute-done | bytes 237600 | tf_op jit(solution)/shard_map/ppermute | solution.py:546
  82.7 0.0 collective-permute-start.8
  82.7 1.5 %collective-permute-done.8.a_other.rest_1_ = f32[464,128]{1,0:T(8,128)S(1)} collective-permute-done((f32[464,128]{1,0:T(8,128)S(1)}, f32[464,128]{1,0:T(8,128)S(1)}, u32[]{:S(2)}, u32[]{:S(2)}) %collective-permute-start.8) | collective-permute-done | bytes 237600 | tf_op jit(solution)/shard_map/ppermute | solution.py:546
  84.2 0.6 pack_corners.3
  84.7 1.0 %collective-permute-done.10.rest_3_ = f32[928,128]{1,0:T(8,128)S(1)} collective-permute-done((f32[928,128]{1,0:T(8,128)S(1)}, f32[928,128]{1,0:T(8,128)S(1)}, u32[]{:S(2)}, u32[]{:S(2)}) %collective-permute-start.10) | collective-permute-done | bytes 475168 | tf_op jit(solution)/shard_map/ppermute | solution.py:546
  85.8 0.0 collective-permute-start.11
  85.8 2.0 %collective-permute-start.12 = (f32[128,128]{1,0:T(8,128)S(1)}, f32[128,128]{1,0:T(8,128)S(1)}, u32[]{:S(2)}, u32[]{:S(2)}) collective-permute-start(f32[128,128]{1,0:T(8,128)S(1)} %pack_corners.3), channel_id=1, source_target_pairs={{0,17},{17,0},{1,18},{18,1},{2,19},{19,2},{3,20},{20,3},{4,21},{21... | collective-permute-start | bytes 196616 | tf_op jit(solution)/shard_map/ppermute | solution.py:546
  87.8 0.0 copy-done.2
  87.8 0.2 multiply_cosine_fusion
  88.0 3.3 %collective-permute-done.12.rest_5_ = f32[128,128]{1,0:T(8,128)S(1)} collective-permute-done((f32[128,128]{1,0:T(8,128)S(1)}, f32[128,128]{1,0:T(8,128)S(1)}, u32[]{:S(2)}, u32[]{:S(2)}) %collective-permute-start.12) | collective-permute-done | bytes 65568 | tf_op jit(solution)/shard_map/ppermute | solution.py:546
  91.4 0.0 collective-permute-start.13
  91.4 1.2 %collective-permute-done.13.rest_6_ = f32[128,128]{1,0:T(8,128)S(1)} collective-permute-done((f32[128,128]{1,0:T(8,128)S(1)}, f32[128,128]{1,0:T(8,128)S(1)}, u32[]{:S(2)}, u32[]{:S(2)}) %collective-permute-start.13) | collective-permute-done | bytes 65568 | tf_op jit(solution)/shard_map/ppermute | solution.py:546
  92.6 0.0 collective-permute-done.11.rest_4_
  92.6 4.8 %adjoint.1 = (f32[3,256,128]{2,1,0:T(8,128)}, f32[3,256,128]{2,1,0:T(8,128)}, f32[2,2,2,8]{3,2,1,0:T(2,128)}) custom-call(s32[3]{0:T(128)S(1)} %pad_add_fusion.ids, f32[6,256,128]{2,1,0:T(8,128)S(1)} %get-tuple-element.35.own, f32[464,128]{1,0:T(8,128)S(1)} %collective-permute-done.7.a.rest_0_, f32[464,128]{1,0:T(8,128)S(1)} %collective-permute-done.8.a_other.rest_1_, ...), custom_call_target="tpu_custom_call" | custom-call | tf_op jit(solution)/shard_map/adjoint/pallas_call | solution.py:528
  (4 shorter events, 0.0 us)
Async XLA Ops:
  4.1 3.5 %collective-permute-start.1 = (f32[2000,128]{1,0:T(8,128)S(1)}, f32[2000,128]{1,0:T(8,128)S(1)}, u32[]{:S(2)}, u32[]{:S(2)}) collective-permute-start(f32[2000,128]{1,0:T(8,128)S(1)} %get-tuple-element.28), channel_id=1, source_target_pairs={{0,16},{16,0},{32,48},{48,32},{64,80},{80,64},{96,112},{112,96},{1... | collective-permute-start | bytes 3072008 | tf_op jit(solution)/shard_map/ppermute | solution.py:546
  4.8 43.4 %collective-permute-start = (f32[1424,128]{1,0:T(8,128)}, f32[1424,128]{1,0:T(8,128)S(1)}, u32[]{:S(2)}, u32[]{:S(2)}) collective-permute-start(f32[1424,128]{1,0:T(8,128)} %get-tuple-element.26), channel_id=1, source_target_pairs={{16,32},{32,16},{48,64},{64,48},{80,96},{96,80},{112,128},{128,112... | collective-permute-start | bytes 2187272 | tf_op jit(solution)/shard_map/ppermute | solution.py:546
  9.3 42.3 %collective-permute-start.3 = (f32[2848,128]{1,0:T(8,128)}, f32[2848,128]{1,0:T(8,128)}, u32[]{:S(2)}, u32[]{:S(2)}) collective-permute-start(f32[2848,128]{1,0:T(8,128)} %pack_rows.2), channel_id=1, source_target_pairs={{0,17},{17,0},{1,18},{18,1},{2,19},{19,2},{3,20},{20,3},{4,21},{21... | collective-permute-start | bytes 4374536 | tf_op jit(solution)/shard_map/ppermute | solution.py:546
  48.2 14.5 %copy-start = (f32[8,8,128]{2,1,0:T(8,128)S(1)}, f32[8,8,128]{2,1,0:T(8,128)}, u32[]{:S(2)}) copy-start(f32[8,8,128]{2,1,0:T(8,128)} %constant.28.clone.rest_8_) | copy-start | bytes 98308
  48.2 14.4 %copy-start.1 = (f32[4]{0:T(128)S(1)}, f32[4]{0:T(128)}, u32[]{:S(2)}) copy-start(f32[4]{0:T(128)} %perm.1) | copy-start | bytes 52
  48.2 2.7 %collective-permute-start.2 = (f32[1424,128]{1,0:T(8,128)S(1)}, f32[1424,128]{1,0:T(8,128)S(1)}, u32[]{:S(2)}, u32[]{:S(2)}) collective-permute-start(f32[1424,128]{1,0:T(8,128)S(1)} %collective-permute-done.a.rest_0_), channel_id=1, source_target_pairs={{0,16},{16,0},{32,48},{48,32},{64,80},{80,64},{96,112},{112,96},{1... | collective-permute-start | bytes 2187272 | tf_op jit(solution)/shard_map/ppermute | solution.py:546
  51.6 11.1 %collective-permute-start.4 = (f32[2848,128]{1,0:T(8,128)}, f32[2848,128]{1,0:T(8,128)S(1)}, u32[]{:S(2)}, u32[]{:S(2)}) collective-permute-start(f32[2848,128]{1,0:T(8,128)} %collective-permute-done.3.rest_3_), channel_id=1, source_target_pairs={{0,16},{16,0},{32,48},{48,32},{64,80},{80,64},{96,112},{112,96},{1... | collective-permute-start | bytes 4374536 | tf_op jit(solution)/shard_map/ppermute | solution.py:546
  52.0 8.9 %collective-permute-start.5 = (f32[736,128]{1,0:T(8,128)S(1)}, f32[736,128]{1,0:T(8,128)S(1)}, u32[]{:S(2)}, u32[]{:S(2)}) collective-permute-start(f32[736,128]{1,0:T(8,128)S(1)} %pack_corners.2), channel_id=1, source_target_pairs={{0,17},{17,0},{1,18},{18,1},{2,19},{19,2},{3,20},{20,3},{4,21},{21... | collective-permute-start | bytes 1130504 | tf_op jit(solution)/shard_map/ppermute | solution.py:546
  61.0 1.7 %collective-permute-start.6 = (f32[736,128]{1,0:T(8,128)S(1)}, f32[736,128]{1,0:T(8,128)S(1)}, u32[]{:S(2)}, u32[]{:S(2)}) collective-permute-start(f32[736,128]{1,0:T(8,128)S(1)} %collective-permute-done.5.rest_5_), channel_id=1, source_target_pairs={{0,16},{16,0},{32,48},{48,32},{64,80},{80,64},{96,112},{112,96},{1... | collective-permute-start | bytes 1130504 | tf_op jit(solution)/shard_map/ppermute | solution.py:546
  72.6 2.6 %collective-permute-start.9 = (f32[760,128]{1,0:T(8,128)S(1)}, f32[760,128]{1,0:T(8,128)S(1)}, u32[]{:S(2)}, u32[]{:S(2)}) collective-permute-start(f32[760,128]{1,0:T(8,128)S(1)} %get-tuple-element.37), channel_id=1, source_target_pairs={{0,16},{16,0},{32,48},{48,32},{64,80},{80,64},{96,112},{112,96},{1... | collective-permute-start | bytes 1167368 | tf_op jit(solution)/shard_map/ppermute | solution.py:546
  72.8 9.8 %collective-permute-start.7 = (f32[464,128]{1,0:T(8,128)S(1)}, f32[464,128]{1,0:T(8,128)S(1)}, u32[]{:S(2)}, u32[]{:S(2)}) collective-permute-start(f32[464,128]{1,0:T(8,128)S(1)} %get-tuple-element.36), channel_id=1, source_target_pairs={{16,32},{32,16},{48,64},{64,48},{80,96},{96,80},{112,128},{128,112... | collective-permute-start | bytes 712712 | tf_op jit(solution)/shard_map/ppermute | solution.py:546
  75.2 12.6 %copy-start.2 = (f32[8]{0:T(128)S(1)}, f32[8]{0:T(128)}, u32[]{:S(2)}) copy-start(f32[8]{0:T(128)} %param.16) | copy-start | bytes 100
  75.8 10.0 %collective-permute-start.10 = (f32[928,128]{1,0:T(8,128)S(1)}, f32[928,128]{1,0:T(8,128)S(1)}, u32[]{:S(2)}, u32[]{:S(2)}) collective-permute-start(f32[928,128]{1,0:T(8,128)S(1)} %pack_rows.3), channel_id=1, source_target_pairs={{0,17},{17,0},{1,18},{18,1},{2,19},{19,2},{3,20},{20,3},{4,21},{21... | collective-permute-start | bytes 1425416 | tf_op jit(solution)/shard_map/ppermute | solution.py:546
  82.7 1.5 %collective-permute-start.8 = (f32[464,128]{1,0:T(8,128)S(1)}, f32[464,128]{1,0:T(8,128)S(1)}, u32[]{:S(2)}, u32[]{:S(2)}) collective-permute-start(f32[464,128]{1,0:T(8,128)S(1)} %collective-permute-done.7.a.rest_0_), channel_id=1, source_target_pairs={{0,16},{16,0},{32,48},{48,32},{64,80},{80,64},{96,112},{112,96},{1... | collective-permute-start | bytes 712712 | tf_op jit(solution)/shard_map/ppermute | solution.py:546
  85.8 6.9 %collective-permute-start.11 = (f32[928,128]{1,0:T(8,128)S(1)}, f32[928,128]{1,0:T(8,128)S(1)}, u32[]{:S(2)}, u32[]{:S(2)}) collective-permute-start(f32[928,128]{1,0:T(8,128)S(1)} %collective-permute-done.10.rest_3_), channel_id=1, source_target_pairs={{0,16},{16,0},{32,48},{48,32},{64,80},{80,64},{96,112},{112,96},{1... | collective-permute-start | bytes 1425416 | tf_op jit(solution)/shard_map/ppermute | solution.py:546
  85.8 5.6 %collective-permute-start.12 = (f32[128,128]{1,0:T(8,128)S(1)}, f32[128,128]{1,0:T(8,128)S(1)}, u32[]{:S(2)}, u32[]{:S(2)}) collective-permute-start(f32[128,128]{1,0:T(8,128)S(1)} %pack_corners.3), channel_id=1, source_target_pairs={{0,17},{17,0},{1,18},{18,1},{2,19},{19,2},{3,20},{20,3},{4,21},{21... | collective-permute-start | bytes 196616 | tf_op jit(solution)/shard_map/ppermute | solution.py:546
  91.4 1.3 %collective-permute-start.13 = (f32[128,128]{1,0:T(8,128)S(1)}, f32[128,128]{1,0:T(8,128)S(1)}, u32[]{:S(2)}, u32[]{:S(2)}) collective-permute-start(f32[128,128]{1,0:T(8,128)S(1)} %collective-permute-done.12.rest_5_), channel_id=1, source_target_pairs={{0,16},{16,0},{32,48},{48,32},{64,80},{80,64},{96,112},{112,96},{1... | collective-permute-start | bytes 196616 | tf_op jit(solution)/shard_map/ppermute | solution.py:546

commit v3 on v2

--- a/solution.py
+++ b/solution.py
@@ -375,7 +375,7 @@
     here = jnp.where(domain == 0, sign[0], 0.0) + jnp.where(domain == 1, sign[1], 0.0)
     mine = jnp.where(lane < 64, before, here)
     for k in range(sent.shape[0]):
-        sent[k, :, :] = mine
+        sent[k, :, :] = mine[0:1, :]
     for f in range(13):
         if f in (0, 3, 6, 7, 10):
             copies[(0, 3, 6, 7, 10).index(f)].wait()
@@ -400,7 +400,7 @@
     both_cores(ids, lambda core: pack_c(core, exchange, own, {"a": a, "a_other": a_other}, "c2", out))
     if len(rest) == 2:
         rows = exchange.rows["c2"]
-        out[rows : rows + 8, :] = rest[0][...]
+        out[rows : rows + 8, :] = jnp.broadcast_to(rest[0][...], (8, LANES))
 
 
 def drive_tables(ids, env_left, env, env_right, beta, alpha, drive):
@@ -445,7 +445,7 @@
     env_c, env_d = (refs[k][EX1.rows["c2"] : EX1.rows["c2"] + 8, :] for k in ("c2", "c2_other"))
     left = jnp.where(ids[0] == 0, env_d, env_c)
     right = jnp.where(ids[0] == 0, env_c, env_d)
-    drive_tables(ids, left, env[...], right, beta, alpha, drive)
+    drive_tables(ids, left, jnp.broadcast_to(env[...], (8, LANES)), right, beta, alpha, drive)
 
     def coefficients(start, group):
         for j in range(group):
@@ -589,7 +589,7 @@
     own, a, b, sent = call(
         kernel_start,
         "start",
-        [(13, CELLS * CELLS, LANES), (EX1.rows["a"], LANES), (EX1.rows["b"], LANES), (n_len, 8, LANES)],
+        [(13, CELLS * CELLS, LANES), (EX1.rows["a"], LANES), (EX1.rows["b"], LANES), (n_len, 1, LANES)],
         [ids, pltpu.with_memory_space_constraint(poling, pltpu.HBM), *[pltpu.with_memory_space_constraint(x, pltpu.HBM) for x in raw]],
         smem=2,
         hbm=range(2, 7),

time: 97.8 us -> 97.4 us (level)
  no operation moved by 1% of the time
where the time goes in v3:
time: 97.4 us; the launch traced here: 97.1 us
  blocking collectives  36.1 us (37%)
  waiting for transfers between devices  22.5 us (23%)
  Pallas kernels  21.6 us (22%)
  starting transfers between devices  15.6 us (16%)
    all_to_all x1, blocking collectives, spread(): env, extra = ([jnp.sum(lax.all_to_all(sent, 'len', 0, 0), axis=0)], 8)  36.1 us
    ppermute x14, waiting for transfers between devices, swap(): lax.ppermute(value, axes, [p for i, j in pairs for p in ((i, j), (j, i))])  22.5 us
    pallas_call x7, Pallas kernels, call(): pl.pallas_call(kernel, out_shape=[jax.ShapeDtypeStruct(s, jnp.float32) fo...  21.6 us
    ppermute x14, starting transfers between devices, swap(): lax.ppermute(value, axes, [p for i, j in pairs for p in ((i, j), (j, i))])  15.6 us
  transfers between devices with their start and end apart: 14, of which 8 were waited for; matrix products, arithmetic and copies ran while one was open for 0% of the time, Pallas kernels for 4%

profile of v3, /device:TPU:229, one launch (start us, length us, event | category | flops | bytes accessed | tf_op | source)
XLA Modules:
  0.0 97.1 jit_solution(13922742928177848371)
XLA Ops:
  0.6 0.1 pad_add_fusion.ids
  0.7 3.3 %start.1 = (f32[13,256,128]{2,1,0:T(8,128)S(1)}, f32[1424,128]{1,0:T(8,128)}, f32[2000,128]{1,0:T(8,128)S(1)}, f32[16,1,128]{2,1,0:T(1,128)S(1)}) custom-call(s32[3]{0:T(128)S(1)} %pad_add_fusion.ids, s32[2,2]{1,0:T(2,128)} %poling.1, f32[3,256,128]{2,1,0:T(8,128)} %bitcast.15, f32[3,256,128]{2,1,0:T(8,128)} %bitcast.16, s32[256,128]{1,0:T(8,128)} %bitcast.19, ...), custom_call_target="tpu_custom_call" | custom-call | tf_op jit(solution)/shard_map/start/pallas_call | solution.py:528
  4.1 0.8 collective-permute-start.1
  4.8 2.7 %collective-permute-start = (f32[1424,128]{1,0:T(8,128)}, f32[1424,128]{1,0:T(8,128)S(1)}, u32[]{:S(2)}, u32[]{:S(2)}) collective-permute-start(f32[1424,128]{1,0:T(8,128)} %get-tuple-element.26), channel_id=1, source_target_pairs={{16,32},{32,16},{48,64},{64,48},{80,96},{96,80},{112,128},{128,112... | collective-permute-start | bytes 2187272 | tf_op jit(solution)/shard_map/ppermute | solution.py:546
  7.5 0.0 collective-permute-done.1.b.rest_2_
  7.6 1.8 %pack_rows.2 = f32[2848,128]{1,0:T(8,128)} custom-call(s32[3]{0:T(128)S(1)} %pad_add_fusion.ids, f32[13,256,128]{2,1,0:T(8,128)S(1)} %get-tuple-element.25.own, f32[2000,128]{1,0:T(8,128)S(1)} %collective-permute-done.1.b.rest_2_), custom_call_target="tpu_custom_call" | custom-call | tf_op jit(solution)/shard_map/pack_rows/pallas_call | solution.py:528
  9.3 2.4 %collective-permute-start.3 = (f32[2848,128]{1,0:T(8,128)}, f32[2848,128]{1,0:T(8,128)}, u32[]{:S(2)}, u32[]{:S(2)}) collective-permute-start(f32[2848,128]{1,0:T(8,128)} %pack_rows.2), channel_id=1, source_target_pairs={{0,17},{17,0},{1,18},{18,1},{2,19},{19,2},{3,20},{20,3},{4,21},{21... | collective-permute-start | bytes 4374536 | tf_op jit(solution)/shard_map/ppermute | solution.py:546
  11.7 36.1 %all_to_all.5 = f32[16,1,128]{2,1,0:T(1,128)S(1)} all-to-all(f32[16,1,128]{2,1,0:T(1,128)S(1)} %get-tuple-element.29), channel_id=1, replica_groups=mesh['len'=16,'wid'=16] {'len'}, dimensions={0} | all-to-all | bytes 16384 | tf_op jit(solution)/shard_map/all_to_all | solution.py:581
  47.9 0.0 collective-permute-done.a.rest_0_
  47.9 0.0 copy-start
  47.9 0.0 copy-start.1
  47.9 0.8 collective-permute-start.2
  48.7 1.8 %collective-permute-done.2.a_other.rest_1_ = f32[1424,128]{1,0:T(8,128)S(1)} collective-permute-done((f32[1424,128]{1,0:T(8,128)S(1)}, f32[1424,128]{1,0:T(8,128)S(1)}, u32[]{:S(2)}, u32[]{:S(2)}) %collective-permute-start.2) | collective-permute-done | bytes 729120 | tf_op jit(solution)/shard_map/ppermute | solution.py:546
  50.5 0.6 pack_corners.2
  51.1 0.0 collective-permute-done.3.rest_3_
  51.1 0.5 collective-permute-start.4
  51.6 1.9 %collective-permute-start.5 = (f32[736,128]{1,0:T(8,128)S(1)}, f32[736,128]{1,0:T(8,128)S(1)}, u32[]{:S(2)}, u32[]{:S(2)}) collective-permute-start(f32[736,128]{1,0:T(8,128)S(1)} %pack_corners.2), channel_id=1, source_target_pairs={{0,17},{17,0},{1,18},{18,1},{2,19},{19,2},{3,20},{20,3},{4,21},{21... | collective-permute-start | bytes 1130504 | tf_op jit(solution)/shard_map/ppermute | solution.py:546
  53.5 7.0 %collective-permute-done.5.rest_5_ = f32[736,128]{1,0:T(8,128)S(1)} collective-permute-done((f32[736,128]{1,0:T(8,128)S(1)}, f32[736,128]{1,0:T(8,128)S(1)}, u32[]{:S(2)}, u32[]{:S(2)}) %collective-permute-start.5) | collective-permute-done | bytes 376864 | tf_op jit(solution)/shard_map/ppermute | solution.py:546
  60.5 0.0 collective-permute-start.6
  60.5 1.7 %collective-permute-done.6.rest_6_ = f32[736,128]{1,0:T(8,128)S(1)} collective-permute-done((f32[736,128]{1,0:T(8,128)S(1)}, f32[736,128]{1,0:T(8,128)S(1)}, u32[]{:S(2)}, u32[]{:S(2)}) %collective-permute-start.6) | collective-permute-done | bytes 376864 | tf_op jit(solution)/shard_map/ppermute | solution.py:546
  62.2 0.0 collective-permute-done.4.rest_4_
  62.2 0.0 copy-done
  62.2 0.0 copy-done.1
  62.2 9.9 %forward.1 = (f32[464,128]{1,0:T(8,128)S(1)}, f32[760,128]{1,0:T(8,128)S(1)}, f32[6,256,128]{2,1,0:T(8,128)S(1)}, f32[1280,128]{1,0:T(8,128)S(1)}, f32[5,3,832,1...) custom-call(s32[3]{0:T(128)S(1)} %pad_add_fusion.ids, f32[4]{0:T(128)S(1)} %copy-done.1, ...), custom_call_target="tpu_custom_call" | custom-call | tf_op jit(solution)/shard_map/forward/pallas_call | solution.py:528
  72.2 0.2 collective-permute-start.9
  72.4 2.4 %collective-permute-start.7 = (f32[464,128]{1,0:T(8,128)S(1)}, f32[464,128]{1,0:T(8,128)S(1)}, u32[]{:S(2)}, u32[]{:S(2)}) collective-permute-start(f32[464,128]{1,0:T(8,128)S(1)} %get-tuple-element.36), channel_id=1, source_target_pairs={{16,32},{32,16},{48,64},{64,48},{80,96},{96,80},{112,128},{128,112... | collective-permute-start | bytes 712712 | tf_op jit(solution)/shard_map/ppermute | solution.py:546
  74.8 0.0 collective-permute-done.9.b.rest_2_
  74.8 0.0 copy-start.2
  74.8 0.6 pack_rows.3
  75.4 1.9 %collective-permute-start.10 = (f32[928,128]{1,0:T(8,128)S(1)}, f32[928,128]{1,0:T(8,128)S(1)}, u32[]{:S(2)}, u32[]{:S(2)}) collective-permute-start(f32[928,128]{1,0:T(8,128)S(1)} %pack_rows.3), channel_id=1, source_target_pairs={{0,17},{17,0},{1,18},{18,1},{2,19},{19,2},{3,20},{20,3},{4,21},{21... | collective-permute-start | bytes 1425416 | tf_op jit(solution)/shard_map/ppermute | solution.py:546
  77.3 4.1 %collective-permute-done.7.a.rest_0_ = f32[464,128]{1,0:T(8,128)S(1)} collective-permute-done((f32[464,128]{1,0:T(8,128)S(1)}, f32[464,128]{1,0:T(8,128)S(1)}, u32[]{:S(2)}, u32[]{:S(2)}) %collective-permute-start.7) | collective-permute-done | bytes 237600 | tf_op jit(solution)/shard_map/ppermute | solution.py:546
  81.4 0.0 collective-permute-start.8
  81.4 1.5 %collective-permute-done.8.a_other.rest_1_ = f32[464,128]{1,0:T(8,128)S(1)} collective-permute-done((f32[464,128]{1,0:T(8,128)S(1)}, f32[464,128]{1,0:T(8,128)S(1)}, u32[]{:S(2)}, u32[]{:S(2)}) %collective-permute-start.8) | collective-permute-done | bytes 237600 | tf_op jit(solution)/shard_map/ppermute | solution.py:546
  82.9 0.6 pack_corners.3
  83.5 1.9 %collective-permute-done.10.rest_3_ = f32[928,128]{1,0:T(8,128)S(1)} collective-permute-done((f32[928,128]{1,0:T(8,128)S(1)}, f32[928,128]{1,0:T(8,128)S(1)}, u32[]{:S(2)}, u32[]{:S(2)}) %collective-permute-start.10) | collective-permute-done | bytes 475168 | tf_op jit(solution)/shard_map/ppermute | solution.py:546
  85.4 0.0 collective-permute-start.11
  85.4 2.0 %collective-permute-start.12 = (f32[128,128]{1,0:T(8,128)S(1)}, f32[128,128]{1,0:T(8,128)S(1)}, u32[]{:S(2)}, u32[]{:S(2)}) collective-permute-start(f32[128,128]{1,0:T(8,128)S(1)} %pack_corners.3), channel_id=1, source_target_pairs={{0,17},{17,0},{1,18},{18,1},{2,19},{19,2},{3,20},{20,3},{4,21},{21... | collective-permute-start | bytes 196616 | tf_op jit(solution)/shard_map/ppermute | solution.py:546
  87.4 0.0 copy-done.2
  87.4 0.2 multiply_cosine_fusion
  87.6 3.3 %collective-permute-done.12.rest_5_ = f32[128,128]{1,0:T(8,128)S(1)} collective-permute-done((f32[128,128]{1,0:T(8,128)S(1)}, f32[128,128]{1,0:T(8,128)S(1)}, u32[]{:S(2)}, u32[]{:S(2)}) %collective-permute-start.12) | collective-permute-done | bytes 65568 | tf_op jit(solution)/shard_map/ppermute | solution.py:546
  91.0 0.0 collective-permute-start.13
  91.0 1.2 %collective-permute-done.13.rest_6_ = f32[128,128]{1,0:T(8,128)S(1)} collective-permute-done((f32[128,128]{1,0:T(8,128)S(1)}, f32[128,128]{1,0:T(8,128)S(1)}, u32[]{:S(2)}, u32[]{:S(2)}) %collective-permute-start.13) | collective-permute-done | bytes 65568 | tf_op jit(solution)/shard_map/ppermute | solution.py:546
  92.2 0.0 collective-permute-done.11.rest_4_
  92.2 4.8 %adjoint.1 = (f32[3,256,128]{2,1,0:T(8,128)}, f32[3,256,128]{2,1,0:T(8,128)}, f32[2,2,2,8]{3,2,1,0:T(2,128)}) custom-call(s32[3]{0:T(128)S(1)} %pad_add_fusion.ids, f32[6,256,128]{2,1,0:T(8,128)S(1)} %get-tuple-element.35.own, f32[464,128]{1,0:T(8,128)S(1)} %collective-permute-done.7.a.rest_0_, f32[464,128]{1,0:T(8,128)S(1)} %collective-permute-done.8.a_other.rest_1_, ...), custom_call_target="tpu_custom_call" | custom-call | tf_op jit(solution)/shard_map/adjoint/pallas_call | solution.py:528
  (4 shorter events, 0.1 us)
Async XLA Ops:
  4.1 3.5 %collective-permute-start.1 = (f32[2000,128]{1,0:T(8,128)S(1)}, f32[2000,128]{1,0:T(8,128)S(1)}, u32[]{:S(2)}, u32[]{:S(2)}) collective-permute-start(f32[2000,128]{1,0:T(8,128)S(1)} %get-tuple-element.28), channel_id=1, source_target_pairs={{0,16},{16,0},{32,48},{48,32},{64,80},{80,64},{96,112},{112,96},{1... | collective-permute-start | bytes 3072008 | tf_op jit(solution)/shard_map/ppermute | solution.py:546
  4.8 43.1 %collective-permute-start = (f32[1424,128]{1,0:T(8,128)}, f32[1424,128]{1,0:T(8,128)S(1)}, u32[]{:S(2)}, u32[]{:S(2)}) collective-permute-start(f32[1424,128]{1,0:T(8,128)} %get-tuple-element.26), channel_id=1, source_target_pairs={{16,32},{32,16},{48,64},{64,48},{80,96},{96,80},{112,128},{128,112... | collective-permute-start | bytes 2187272 | tf_op jit(solution)/shard_map/ppermute | solution.py:546
  9.3 41.8 %collective-permute-start.3 = (f32[2848,128]{1,0:T(8,128)}, f32[2848,128]{1,0:T(8,128)}, u32[]{:S(2)}, u32[]{:S(2)}) collective-permute-start(f32[2848,128]{1,0:T(8,128)} %pack_rows.2), channel_id=1, source_target_pairs={{0,17},{17,0},{1,18},{18,1},{2,19},{19,2},{3,20},{20,3},{4,21},{21... | collective-permute-start | bytes 4374536 | tf_op jit(solution)/shard_map/ppermute | solution.py:546
  47.9 14.4 %copy-start = (f32[8,8,128]{2,1,0:T(8,128)S(1)}, f32[8,8,128]{2,1,0:T(8,128)}, u32[]{:S(2)}) copy-start(f32[8,8,128]{2,1,0:T(8,128)} %constant.28.clone.rest_8_) | copy-start | bytes 98308
  47.9 14.3 %copy-start.1 = (f32[4]{0:T(128)S(1)}, f32[4]{0:T(128)}, u32[]{:S(2)}) copy-start(f32[4]{0:T(128)} %perm.1) | copy-start | bytes 52
  47.9 2.6 %collective-permute-start.2 = (f32[1424,128]{1,0:T(8,128)S(1)}, f32[1424,128]{1,0:T(8,128)S(1)}, u32[]{:S(2)}, u32[]{:S(2)}) collective-permute-start(f32[1424,128]{1,0:T(8,128)S(1)} %collective-permute-done.a.rest_0_), channel_id=1, source_target_pairs={{0,16},{16,0},{32,48},{48,32},{64,80},{80,64},{96,112},{112,96},{1... | collective-permute-start | bytes 2187272 | tf_op jit(solution)/shard_map/ppermute | solution.py:546
  51.1 11.1 %collective-permute-start.4 = (f32[2848,128]{1,0:T(8,128)}, f32[2848,128]{1,0:T(8,128)S(1)}, u32[]{:S(2)}, u32[]{:S(2)}) collective-permute-start(f32[2848,128]{1,0:T(8,128)} %collective-permute-done.3.rest_3_), channel_id=1, source_target_pairs={{0,16},{16,0},{32,48},{48,32},{64,80},{80,64},{96,112},{112,96},{1... | collective-permute-start | bytes 4374536 | tf_op jit(solution)/shard_map/ppermute | solution.py:546
  51.6 8.9 %collective-permute-start.5 = (f32[736,128]{1,0:T(8,128)S(1)}, f32[736,128]{1,0:T(8,128)S(1)}, u32[]{:S(2)}, u32[]{:S(2)}) collective-permute-start(f32[736,128]{1,0:T(8,128)S(1)} %pack_corners.2), channel_id=1, source_target_pairs={{0,17},{17,0},{1,18},{18,1},{2,19},{19,2},{3,20},{20,3},{4,21},{21... | collective-permute-start | bytes 1130504 | tf_op jit(solution)/shard_map/ppermute | solution.py:546
  60.5 1.7 %collective-permute-start.6 = (f32[736,128]{1,0:T(8,128)S(1)}, f32[736,128]{1,0:T(8,128)S(1)}, u32[]{:S(2)}, u32[]{:S(2)}) collective-permute-start(f32[736,128]{1,0:T(8,128)S(1)} %collective-permute-done.5.rest_5_), channel_id=1, source_target_pairs={{0,16},{16,0},{32,48},{48,32},{64,80},{80,64},{96,112},{112,96},{1... | collective-permute-start | bytes 1130504 | tf_op jit(solution)/shard_map/ppermute | solution.py:546
  72.2 2.6 %collective-permute-start.9 = (f32[760,128]{1,0:T(8,128)S(1)}, f32[760,128]{1,0:T(8,128)S(1)}, u32[]{:S(2)}, u32[]{:S(2)}) collective-permute-start(f32[760,128]{1,0:T(8,128)S(1)} %get-tuple-element.37), channel_id=1, source_target_pairs={{0,16},{16,0},{32,48},{48,32},{64,80},{80,64},{96,112},{112,96},{1... | collective-permute-start | bytes 1167368 | tf_op jit(solution)/shard_map/ppermute | solution.py:546
  72.4 9.0 %collective-permute-start.7 = (f32[464,128]{1,0:T(8,128)S(1)}, f32[464,128]{1,0:T(8,128)S(1)}, u32[]{:S(2)}, u32[]{:S(2)}) collective-permute-start(f32[464,128]{1,0:T(8,128)S(1)} %get-tuple-element.36), channel_id=1, source_target_pairs={{16,32},{32,16},{48,64},{64,48},{80,96},{96,80},{112,128},{128,112... | collective-permute-start | bytes 712712 | tf_op jit(solution)/shard_map/ppermute | solution.py:546
  74.8 12.6 %copy-start.2 = (f32[8]{0:T(128)S(1)}, f32[8]{0:T(128)}, u32[]{:S(2)}) copy-start(f32[8]{0:T(128)} %param.16) | copy-start | bytes 100
  75.4 10.0 %collective-permute-start.10 = (f32[928,128]{1,0:T(8,128)S(1)}, f32[928,128]{1,0:T(8,128)S(1)}, u32[]{:S(2)}, u32[]{:S(2)}) collective-permute-start(f32[928,128]{1,0:T(8,128)S(1)} %pack_rows.3), channel_id=1, source_target_pairs={{0,17},{17,0},{1,18},{18,1},{2,19},{19,2},{3,20},{20,3},{4,21},{21... | collective-permute-start | bytes 1425416 | tf_op jit(solution)/shard_map/ppermute | solution.py:546
  81.4 1.5 %collective-permute-start.8 = (f32[464,128]{1,0:T(8,128)S(1)}, f32[464,128]{1,0:T(8,128)S(1)}, u32[]{:S(2)}, u32[]{:S(2)}) collective-permute-start(f32[464,128]{1,0:T(8,128)S(1)} %collective-permute-done.7.a.rest_0_), channel_id=1, source_target_pairs={{0,16},{16,0},{32,48},{48,32},{64,80},{80,64},{96,112},{112,96},{1... | collective-permute-start | bytes 712712 | tf_op jit(solution)/shard_map/ppermute | solution.py:546
  85.4 6.9 %collective-permute-start.11 = (f32[928,128]{1,0:T(8,128)S(1)}, f32[928,128]{1,0:T(8,128)S(1)}, u32[]{:S(2)}, u32[]{:S(2)}) collective-permute-start(f32[928,128]{1,0:T(8,128)S(1)} %collective-permute-done.10.rest_3_), channel_id=1, source_target_pairs={{0,16},{16,0},{32,48},{48,32},{64,80},{80,64},{96,112},{112,96},{1... | collective-permute-start | bytes 1425416 | tf_op jit(solution)/shard_map/ppermute | solution.py:546
  85.4 5.6 %collective-permute-start.12 = (f32[128,128]{1,0:T(8,128)S(1)}, f32[128,128]{1,0:T(8,128)S(1)}, u32[]{:S(2)}, u32[]{:S(2)}) collective-permute-start(f32[128,128]{1,0:T(8,128)S(1)} %pack_corners.3), channel_id=1, source_target_pairs={{0,17},{17,0},{1,18},{18,1},{2,19},{19,2},{3,20},{20,3},{4,21},{21... | collective-permute-start | bytes 196616 | tf_op jit(solution)/shard_map/ppermute | solution.py:546
  91.0 1.3 %collective-permute-start.13 = (f32[128,128]{1,0:T(8,128)S(1)}, f32[128,128]{1,0:T(8,128)S(1)}, u32[]{:S(2)}, u32[]{:S(2)}) collective-permute-start(f32[128,128]{1,0:T(8,128)S(1)} %collective-permute-done.12.rest_5_), channel_id=1, source_target_pairs={{0,16},{16,0},{32,48},{48,32},{64,80},{80,64},{96,112},{112,96},{1... | collective-permute-start | bytes 196616 | tf_op jit(solution)/shard_map/ppermute | solution.py:546
